TPU v7x, 32 devices: a whole 2x2x4 slice. The times are simulated.
32 devices in a mesh: wide: 8 (over z, x), narrow: 4 (over y, core).
Axes of the slice: x: 2, y: 2, z: 4, core: 2. Of those that a mesh axis runs over, the one named last changes fastest.
Arguments:
- features: bfloat16 [18816, 2048], P('wide', 'narrow')
- image_side: int32 [384], P('wide'), may hold values from 5 to 7, as said below
- bank_slot: int32 [384], P('wide'), may hold values from 0 to 32767, as said below
- memory_bank: float32 [32768, 128], P('wide'), may hold values from -0.6 to 0.6
- weight_one: bfloat16 [2048, 512], P(None, 'narrow'), may hold values from -0.125 to 0.125
- gain_one: bfloat16 [512], P('narrow'), may hold values from 0.5 to 1.5
- shift_one: bfloat16 [512], P('narrow'), may hold values from -2 to 2
- weight_two: bfloat16 [3, 3, 512, 512], P(None, None, None, 'narrow'), may hold values from -0.09375 to 0.09375
- gain_two: bfloat16 [512], P('narrow'), may hold values from 0.5 to 1.5
- shift_two: bfloat16 [512], P('narrow'), may hold values from -2 to 2
- weight_three: bfloat16 [512, 2048], P(None, 'narrow'), may hold values from -0.25 to 0.25
- gain_three: bfloat16 [2048], P('narrow'), may hold values from 0.5 to 1.5
- shift_three: bfloat16 [2048], P('narrow'), may hold values from -2 to 2
- weight_head: bfloat16 [2048, 128], P('narrow'), may hold values from -0.125 to 0.125
- out_grad: bfloat16 [18816, 2048], P('wide', 'narrow'), may hold values from -6 to 6
- embed_grad: float32 [384, 128], P('wide'), may hold values from -6 to 6
Outputs:
- out: bfloat16 [18816, 2048], P('wide', 'narrow')
- embedding: float32 [384, 128], P('wide')
- grad_features: bfloat16 [18816, 2048], P('wide', 'narrow')
- grad_weight_one: float32 [2048, 512], P(None, 'narrow')
- grad_gain_one: float32 [512], P('narrow')
- grad_shift_one: float32 [512], P('narrow')
- grad_weight_two: float32 [3, 3, 512, 512], P(None, None, None, 'narrow')
- grad_gain_two: float32 [512], P('narrow')
- grad_shift_two: float32 [512], P('narrow')
- grad_weight_three: float32 [512, 2048], P(None, 'narrow')
- grad_gain_three: float32 [2048], P('narrow')
- grad_shift_three: float32 [2048], P('narrow')
- grad_weight_head: float32 [2048, 128], P('narrow')
- new_bank: float32 [32768, 128], P('wide')
Inputs may be any that keep to these rules, and one draw needn't show every extreme that they name: `image_side`: all images of one index of wide have the same side. `bank_slot`: the 384 rows are all different.
All inputs are finite; a program needn't handle non-finite values.
Results may differ from a plain program's by a relative error of at most 0.009.
Values may be sent and summed in bfloat16 or wider, within the bound.
No kernel may reach another device: no remote copies, remote signals or barrier semaphores. Data moves between devices by JAX's collectives and lax.ppermute only.
A program may use at most 192 MiB of HBM per device.

v0:
```python
import jax
import jax.numpy as jnp
from jax import lax
from jax.sharding import PartitionSpec as P

SIDE = 7


EPS_NORM = 1e-05
EPS_EMBED = 1e-06


def pixel_mask(image_side):
    position = jnp.arange(SIDE * SIDE, dtype=jnp.int32)
    row_index = position // SIDE
    column_index = position % SIDE
    inside = (row_index[None, :] < image_side[:, None]) & (
        column_index[None, :] < image_side[:, None]
    )
    return inside.astype(jnp.float32).reshape(-1, 1)


def silu_slope(value):
    sigma = jax.nn.sigmoid(value)
    return sigma * (1.0 + value * (1.0 - sigma))


def gather_narrow(value):
    return lax.all_gather(value, "narrow", axis=1, tiled=True)


def reduce_narrow(value):
    return lax.psum_scatter(value, "narrow", scatter_dimension=1, tiled=True)


def sums_wide(values):
    return lax.psum(values, "wide")


def back_wide(values):
    return lax.psum(values, "wide")


def head_narrow(value):
    return lax.psum(value, "narrow")


def first_scatter(low_one, weight_one):
    partial_value = jnp.einsum("pd,cd->pc", low_one, weight_one, preferred_element_type=jnp.float32)
    return lax.psum_scatter(
        partial_value.astype(jnp.bfloat16), "narrow", scatter_dimension=1, tiled=True
    ).astype(jnp.float32)


def norm_forward(value, gain, shift, mask, local_count, sums_fn):
    total, square, count = sums_fn(
        (jnp.sum(value * mask, axis=0), jnp.sum(value * value * mask, axis=0), local_count)
    )
    mean = total / count
    variance = square / count - mean * mean
    scale = lax.rsqrt(variance + EPS_NORM)
    normal = (value - mean) * scale
    return (gain.astype(jnp.float32) * normal + shift.astype(jnp.float32), normal, scale, count)


def norm_backward(grad_z, normal, gain, scale, count, mask, sums_fn):
    d_shift, d_gain = sums_fn((jnp.sum(grad_z, axis=0), jnp.sum(grad_z * normal, axis=0)))
    grad_y = (
        gain.astype(jnp.float32)
        * scale
        * (grad_z - d_shift / count - normal * d_gain / count)
        * mask
    )
    return (grad_y.astype(jnp.bfloat16), d_gain, d_shift)


def padded_grid(whole, images):
    channels = whole.shape[1]
    grid = whole.reshape(images, SIDE, SIDE, channels)
    return jnp.pad(grid, ((0, 0), (1, 1), (1, 1), (0, 0)))


def conv_forward(whole, weight_two, images):
    channels = whole.shape[1]
    padded = padded_grid(whole, images)
    total = jnp.zeros((whole.shape[0], weight_two.shape[3]), jnp.float32)
    for row_shift in range(3):
        for column_shift in range(3):
            window = padded[
                :, row_shift : row_shift + SIDE, column_shift : column_shift + SIDE
            ].reshape(-1, channels)
            total = total + jnp.dot(
                window, weight_two[row_shift, column_shift], preferred_element_type=jnp.float32
            )
    return total


def conv_backward(whole, grad_low, weight_two, images):
    channels = whole.shape[1]
    padded = padded_grid(whole, images)
    grad_pad = jnp.zeros((images, SIDE + 2, SIDE + 2, channels), jnp.float32)
    weight_rows = []
    for row_shift in range(3):
        row_terms = []
        for column_shift in range(3):
            window = padded[
                :, row_shift : row_shift + SIDE, column_shift : column_shift + SIDE
            ].reshape(-1, channels)
            row_terms.append(
                jnp.einsum("pc,pd->cd", window, grad_low, preferred_element_type=jnp.float32)
            )
            spread_back = jnp.einsum(
                "pd,cd->pc",
                grad_low,
                weight_two[row_shift, column_shift],
                preferred_element_type=jnp.float32,
            )
            grad_pad = grad_pad.at[
                :, row_shift : row_shift + SIDE, column_shift : column_shift + SIDE
            ].add(spread_back.reshape(images, SIDE, SIDE, channels))
        weight_rows.append(jnp.stack(row_terms))
    return (jnp.stack(weight_rows), grad_pad[:, 1 : SIDE + 1, 1 : SIDE + 1].reshape(-1, channels))


def block(
    masked,
    mask,
    counts_img,
    images,
    weights,
    grad_rows,
    embed_rows,
    gather_fn,
    reduce_fn,
    sums_fn,
    back_fn,
    head_fn,
    first_fn,
):
    (
        weight_one,
        weight_two,
        weight_three,
        weight_head,
        gain_one,
        shift_one,
        gain_two,
        shift_two,
        gain_three,
        shift_three,
    ) = weights
    local_count = jnp.sum(counts_img)
    whole_x = gather_fn(masked)
    y_one = jnp.dot(whole_x, weight_one, preferred_element_type=jnp.float32)
    z_one, normal_one, scale_one, count = norm_forward(
        y_one, gain_one, shift_one, mask, local_count, sums_fn
    )
    a_one = (jax.nn.silu(z_one) * mask).astype(jnp.bfloat16)
    whole_one = gather_fn(a_one)
    y_two = conv_forward(whole_one, weight_two, images)
    z_two, normal_two, scale_two, count = norm_forward(
        y_two, gain_two, shift_two, mask, local_count, sums_fn
    )
    a_two = (jax.nn.silu(z_two) * mask).astype(jnp.bfloat16)
    whole_two = gather_fn(a_two)
    y_three = jnp.dot(whole_two, weight_three, preferred_element_type=jnp.float32)
    z_three, normal_three, scale_three, count = norm_forward(
        y_three, gain_three, shift_three, mask, local_count, sums_fn
    )
    summed = z_three + masked.astype(jnp.float32)
    out_full = jax.nn.silu(summed) * mask
    channels = out_full.shape[1]
    pooled = jnp.sum(out_full.reshape(images, SIDE * SIDE, channels), axis=1) / counts_img[:, None]
    pooled_low = pooled.astype(jnp.bfloat16)
    raw = head_fn(jnp.dot(pooled_low, weight_head, preferred_element_type=jnp.float32))
    inverse = lax.rsqrt(jnp.sum(raw * raw, axis=1, keepdims=True) + EPS_EMBED)
    embedding = raw * inverse
    grad_raw = inverse * (
        embed_rows - embedding * jnp.sum(embedding * embed_rows, axis=1, keepdims=True)
    )
    grad_raw_low = grad_raw.astype(jnp.bfloat16)
    grad_head = jnp.einsum(
        "ic,ie->ce", pooled_low, grad_raw_low, preferred_element_type=jnp.float32
    )
    grad_pooled = jnp.einsum(
        "ie,ce->ic", grad_raw_low, weight_head, preferred_element_type=jnp.float32
    )
    spread = jnp.broadcast_to(
        (grad_pooled / counts_img[:, None])[:, None, :], (images, SIDE * SIDE, channels)
    ).reshape(-1, channels)
    grad_summed = (grad_rows.astype(jnp.float32) + spread) * silu_slope(summed) * mask
    low_three, d_gain_three, d_shift_three = norm_backward(
        grad_summed, normal_three, gain_three, scale_three, count, mask, back_fn
    )
    grad_weight_three = jnp.einsum(
        "pc,pd->cd", whole_two, low_three, preferred_element_type=jnp.float32
    )
    grad_a_two = reduce_fn(
        jnp.einsum("pd,cd->pc", low_three, weight_three, preferred_element_type=jnp.float32)
    )
    grad_z_two = grad_a_two * silu_slope(z_two) * mask
    low_two, d_gain_two, d_shift_two = norm_backward(
        grad_z_two, normal_two, gain_two, scale_two, count, mask, back_fn
    )
    grad_weight_two, partial_two = conv_backward(whole_one, low_two, weight_two, images)
    grad_a_one = reduce_fn(partial_two)
    grad_z_one = grad_a_one * silu_slope(z_one) * mask
    low_one, d_gain_one, d_shift_one = norm_backward(
        grad_z_one, normal_one, gain_one, scale_one, count, mask, back_fn
    )
    grad_weight_one = jnp.einsum("pc,pd->cd", whole_x, low_one, preferred_element_type=jnp.float32)
    grad_input = first_fn(low_one, weight_one) + grad_summed
    weight_terms = (grad_weight_one, grad_weight_two, grad_weight_three, grad_head)
    norm_terms = (d_gain_one, d_shift_one, d_gain_two, d_shift_two, d_gain_three, d_shift_three)
    return (out_full, embedding, grad_input, weight_terms, norm_terms)


def shards(
    features,
    image_side,
    bank_slot,
    memory_bank,
    weight_one,
    gain_one,
    shift_one,
    weight_two,
    gain_two,
    shift_two,
    weight_three,
    gain_three,
    shift_three,
    weight_head,
    out_grad,
    embed_grad,
):
    weights = (
        weight_one,
        weight_two,
        weight_three,
        weight_head,
        gain_one,
        shift_one,
        gain_two,
        shift_two,
        gain_three,
        shift_three,
    )
    img_dev = image_side.shape[0]
    mask = pixel_mask(image_side)
    counts_img = (image_side * image_side).astype(jnp.float32)
    masked = features * mask.astype(jnp.bfloat16)
    out_full, embedding, grad_input, weight_terms, norm_terms = block(
        masked,
        mask,
        counts_img,
        img_dev,
        weights,
        out_grad,
        embed_grad,
        gather_narrow,
        reduce_narrow,
        sums_wide,
        back_wide,
        head_narrow,
        first_scatter,
    )
    out_local = out_full.astype(jnp.bfloat16)
    grad_local = grad_input.astype(jnp.bfloat16)
    all_embed, all_slot = (
        lax.all_gather(embedding, "wide", axis=0, tiled=True),
        lax.all_gather(bank_slot.astype(jnp.float32), "wide", axis=0, tiled=True),
    )
    weight_terms = lax.psum(
        (weight_terms[0], weight_terms[1], weight_terms[2], weight_terms[3]), "wide"
    )
    bank_rows_here = memory_bank.shape[0]
    owner_rows = all_slot.astype(jnp.int32) - lax.axis_index("wide") * bank_rows_here
    owned = (owner_rows >= 0) & (owner_rows < bank_rows_here)
    target = jnp.where(owned, owner_rows, bank_rows_here)
    previous = jnp.take(memory_bank, jnp.minimum(target, bank_rows_here - 1), axis=0)
    mixed = 0.5 * previous + 0.5 * all_embed
    mixed = mixed * lax.rsqrt(jnp.sum(mixed * mixed, axis=1, keepdims=True) + EPS_EMBED)
    new_bank = memory_bank.at[target].set(mixed, mode="drop")
    return (
        out_local,
        embedding,
        grad_local,
        weight_terms[0],
        norm_terms[0],
        norm_terms[1],
        weight_terms[1],
        norm_terms[2],
        norm_terms[3],
        weight_terms[2],
        norm_terms[4],
        norm_terms[5],
        weight_terms[3],
        new_bank,
    )


def solution(mesh):
    in_specs = (
        P("wide", "narrow"),
        P("wide"),
        P("wide"),
        P("wide", None),
        P(None, "narrow"),
        P("narrow"),
        P("narrow"),
        P(None, None, None, "narrow"),
        P("narrow"),
        P("narrow"),
        P(None, "narrow"),
        P("narrow"),
        P("narrow"),
        P("narrow", None),
        P("wide", "narrow"),
        P("wide", None),
    )
    out_specs = (
        P("wide", "narrow"),
        P("wide", None),
        P("wide", "narrow"),
        P(None, "narrow"),
        P("narrow"),
        P("narrow"),
        P(None, None, None, "narrow"),
        P("narrow"),
        P("narrow"),
        P(None, "narrow"),
        P("narrow"),
        P("narrow"),
        P("narrow", None),
        P("wide", None),
    )
    return jax.shard_map(shards, mesh=mesh, in_specs=in_specs, out_specs=out_specs, check_vma=False)
```

profile of v0, /device:TPU:0, one launch (start us, length us, event | category | flops | bytes accessed | tf_op | source)
XLA Modules:
  0.0 795.2 jit_solution(212986425749671084)
XLA Ops:
  7.3 3.2 copy.92
  10.7 1.8 broadcast_multiply_fusion
  13.8 67.0 %all-gather.4.cloned.1.call-done = bf16[2352,2048]{1,0:T(8,128)(2,1)} async-done(((bf16[2352,512]{1,0:T(8,128)(2,1)}), bf16[2352,2048]{1,0:T(8,128)(2,1)}) %all-gather.4.cloned.1.call-update) | async-done | bytes 9633808 | tf_op jit(solution)/shard_map/all_gather | solution.py:29
  80.8 5.5 multiply_reduce_fusion.7
  86.3 22.0 %all-reduce.8 = (f32[128]{0:T(128)S(1)}, f32[]{:T(128)}, f32[128]{0:T(128)S(1)}) all-reduce(f32[128]{0:T(128)S(1)} %get-tuple-element.129, f32[]{:T(128)} %fusion.48, f32[128]{0:T(128)S(1)} %get-tuple-element.128), channel_id=1, replica_groups=mesh['wide'=8,'narrow'=4] {'wide'}, use_global_device_ids=true, to_apply=%region_1.2 | all-reduce | flops 257 | bytes 2056 | tf_op jit(solution)/shard_map/psum | solution.py:37
  109.3 1.3 multiply_convert_fusion.4
  111.3 20.5 %all-gather.6.cloned.1.call-done = bf16[2352,512]{1,0:T(8,128)(2,1)} async-done(((bf16[2352,128]{1,0:T(8,128)(2,1)}), bf16[2352,512]{1,0:T(8,128)(2,1)}) %all-gather.6.cloned.1.call-update) | async-done | bytes 2408464 | tf_op jit(solution)/shard_map/all_gather | solution.py:29
  131.7 4.9 reshape.569
  136.7 15.0 %pad_slice_fusion = (bf16[48,7,7,512]{3,2,1,0:T(8,128)(2,1)}, bf16[48,7,7,512]{3,2,1,0:T(8,128)(2,1)}, bf16[48,7,7,512]{3,2,1,0:T(8,128)(2,1)}, bf16[48,7,7,512]...) fusion(bf16[48,7,7,512]{3,2,1,0:T(8,128)(2,1)} %reshape.569), kind=kLoop, calls=%fused_computation.2 | loop fusion | bytes 21676032 | tf_op jit(solution)/shard_map/slice | solution.py:89
  151.7 5.0 reshape.577
  156.7 5.0 reshape.571
  161.6 5.0 reshape.572
  166.6 5.0 reshape.573
  171.6 2.3 reshape.574
  173.9 3.7 reshape.575
  177.6 5.3 reshape.576
  182.9 5.0 reshape.570
  187.9 2.6 fusion.27
  202.4 21.7 %all-reduce.7 = (f32[128]{0:T(128)S(1)}, f32[128]{0:T(128)S(1)}) all-reduce(f32[128]{0:T(128)S(1)} %get-tuple-element.127, f32[128]{0:T(128)S(1)} %get-tuple-element.126), channel_id=1, replica_groups=mesh['wide'=8,'narrow'=4] {'wide'}, use_global_device_ids=true, to_apply=%region_7.8 | all-reduce | flops 256 | bytes 2048 | tf_op jit(solution)/shard_map/psum | solution.py:37
  225.1 1.3 multiply_convert_fusion.3
  226.6 21.0 %all-gather.8.cloned.1.call-done = bf16[2352,512]{1,0:T(8,128)(2,1)} async-done(((bf16[2352,128]{1,0:T(8,128)(2,1)}), bf16[2352,512]{1,0:T(8,128)(2,1)}) %all-gather.8.cloned.1.call-update) | async-done | bytes 2408464 | tf_op jit(solution)/shard_map/all_gather | solution.py:29
  247.5 5.5 multiply_reduce_fusion.2
  253.1 21.3 %all-reduce.6 = (f32[512]{0:T(512)S(1)}, f32[512]{0:T(512)S(1)}) all-reduce(f32[512]{0:T(512)S(1)} %get-tuple-element.123, f32[512]{0:T(512)S(1)} %get-tuple-element.122), channel_id=1, replica_groups=mesh['wide'=8,'narrow'=4] {'wide'}, use_global_device_ids=true, to_apply=%region_13.14 | all-reduce | flops 1024 | bytes 8192 | tf_op jit(solution)/shard_map/psum | solution.py:37
  275.5 6.0 fusion.63
  281.5 5.8 reshape.578
  287.3 4.0 reduce_sum.160
  291.3 1.1 fusion.50
  292.5 10.4 %psum.139 = f32[48,128]{1,0:T(8,128)S(1)} all-reduce(f32[48,128]{1,0:T(8,128)S(1)} %fusion.50), channel_id=1, replica_groups=mesh['wide'=8,'narrow'=4] {'narrow'}, use_global_device_ids=true, to_apply=%region_15.16 | all-reduce | flops 6144 | bytes 49152 | tf_op jit(solution)/shard_map/psum | solution.py:45
  305.9 3.1 broadcast_in_dim.14
  308.9 6.0 reshape.579
  314.9 8.3 %fusion.60 = (f32[512]{0:T(512)S(1)}, f32[512]{0:T(512)S(1)}, f32[2352,512]{1,0:T(8,128)}) fusion(f32[512]{0:T(512)S(1)} %get-tuple-element.163, f32[2352,512]{1,0:T(8,128)} %get-tuple-element.184, f32[512]{0:T(512)S(1)} %get-tuple-element.177, f32[2352]{0:T(1024)S(1)} %reshape.585, f32[512]{0:T(512)S(1)} %convert_element_type.105, ...), kind=kLoop, calls=%fused_computation.170 | loop fusion | flops 25287680 | bytes 19293984 | tf_op jit(solution)/shard_map/reduce_sum | solution.py:67
  323.1 17.1 %all-reduce.5 = (f32[512]{0:T(512)S(1)}, f32[512]{0:T(512)S(1)}) all-reduce(f32[512]{0:T(512)S(1)} %get-tuple-element.125, f32[512]{0:T(512)S(1)} %get-tuple-element.124), channel_id=1, replica_groups=mesh['wide'=8,'narrow'=4] {'wide'}, use_global_device_ids=true, to_apply=%region_21.22 | all-reduce | flops 1024 | bytes 8192 | tf_op jit(solution)/shard_map/psum | solution.py:41
  340.8 5.2 multiply_convert_fusion
  346.1 1.4 copy-done.22
  347.5 3.7 fusion.66
  353.3 44.4 %reduce-scatter.4.cloned.1.call-done = f32[2352,128]{1,0:T(8,128)} async-done(((f32[2352,512]{1,0:T(8,128)}), f32[2352,128]{1,0:T(8,128)}) %reduce-scatter.4.cloned.1.call-update) | async-done | bytes 1204240 | tf_op jit(solution)/shard_map/reduce_scatter | solution.py:33
  397.7 2.0 fusion.62
  399.7 21.8 %all-reduce.4 = (f32[128]{0:T(128)}, f32[128]{0:T(128)S(1)}) all-reduce(f32[128]{0:T(128)S(1)} %get-tuple-element.133, f32[128]{0:T(128)S(1)} %get-tuple-element.132), channel_id=1, replica_groups=mesh['wide'=8,'narrow'=4] {'wide'}, use_global_device_ids=true, to_apply=%region_26.27 | all-reduce | flops 256 | bytes 2048 | tf_op jit(solution)/shard_map/psum | solution.py:41
  422.1 1.6 multiply_convert_fusion.2
  423.9 1.7 fusion.17
  425.6 1.3 scatter-add.30
  426.9 2.4 add_dynamic-update-slice_fusion
  429.3 3.1 fusion
  438.8 5.4 copy.49
  444.2 6.4 reshape.584
  453.2 42.4 %reduce-scatter.6.cloned.1.call-done = f32[2352,128]{1,0:T(8,128)} async-done(((f32[2352,512]{1,0:T(8,128)}), f32[2352,128]{1,0:T(8,128)}) %reduce-scatter.6.cloned.1.call-update) | async-done | bytes 1204240 | tf_op jit(solution)/shard_map/reduce_scatter | solution.py:33
  495.6 2.5 fusion.61
  498.1 22.1 %all-reduce.3 = (f32[128]{0:T(128)}, f32[128]{0:T(128)}, f32[384]{0:T(512)}) all-reduce(f32[128]{0:T(128)} %get-tuple-element.131, f32[128]{0:T(128)} %get-tuple-element.130, f32[384]{0:T(512)} %copy-done.48), channel_id=1, replica_groups=mesh['wide'=8,'narrow'=4] {'wide'}, use_global_device_ids=true, to_apply=%region_32.33 | all-reduce | flops 640 | bytes 5120 | tf_op jit(solution)/shard_map/psum | solution.py:41
  520.1 1.2 broadcast_divide_fusion.2
  521.3 1.6 multiply_convert_fusion.1
  523.8 5.1 convolution_convert_fusion
  529.5 1.9 fusion.49
  531.5 4.4 fusion.68
  536.8 1.4 copy-done.12
  539.0 1.4 copy-done.15
  550.3 1.6 pad_maximum_fusion
  551.9 7.6 fusion.67
  560.3 31.2 %all_gather.19 = f32[384,128]{1,0:T(8,128)S(1)} all-gather(f32[48,128]{1,0:T(8,128)S(1)} %copy-done.36), channel_id=1, replica_groups=mesh['wide'=8,'narrow'=4] {'wide'}, dimensions={0}, use_global_device_ids=true | all-gather | bytes 221184 | tf_op jit(solution)/shard_map/all_gather | solution.py:270
  592.9 2.4 scatter_custom_fusion
  595.3 9.7 %reduce-scatter.8.cloned.1.call-done = bf16[2352,512]{1,0:T(8,128)(2,1)} async-done(((bf16[2352,2048]{1,0:T(8,128)(2,1)}), bf16[2352,512]{1,0:T(8,128)(2,1)}) %reduce-scatter.8.cloned.1.call-update) | async-done | bytes 2408464 | tf_op jit(solution)/shard_map/reduce_scatter | solution.py:50
  605.0 5.4 add_convert_fusion
  610.4 170.5 %all-reduce.12.cloned.1.call-done = (f32[2048,128]{1,0:T(8,128)}, f32[3,3,512,128]{3,2,1,0:T(8,128)}, f32[512,512]{1,0:T(8,128)}, f32[512,128]{1,0:T(8,128)}) async-done(((f32[2048,128]{1,0:T(8,128)}, f32[3,3,512,128]{3,2,1,0:T(8,128)}, f32[512,512]{1,0:T(8,128)}, f32[512,128]{1,0:T(8,128)}), (f32[2048,128]{1,0:T(8,128)}, f32[3,3,512,128]{3,2,1,0:T(8,128)}, f32[512,512]{1,0:T(8,128)}, ...) | async-done | bytes 4718608 | tf_op jit(solution)/shard_map/psum | solution.py:273
  780.8 2.3 copy.93
  783.1 3.3 copy.94
  (219 shorter events, 48.7 us)
Async XLA Ops:
  7.2 73.6 %copy-start = (bf16[2048,128]{1,0:T(8,128)(2,1)S(1)}, bf16[2048,128]{1,0:T(8,128)(2,1)}, u32[]{:S(2)}) copy-start(bf16[2048,128]{1,0:T(8,128)(2,1)} %param.38) | copy-start | bytes 1572868
  7.2 3.3 copy-start.64
  7.2 3.5 copy-start.18
  7.2 73.5 %all-gather.4.cloned.1.call-start = ((), (), s32[]{:S(2)}) async-start(), calls=%async_computation.3 | async-start | bytes 12042240 | tf_op jit(solution)/shard_map/all_gather | solution.py:29
  12.5 119.2 %all-gather.6.cloned.1.call-start = ((), (), s32[]{:S(2)}) async-start(), calls=%async_computation.4 | async-start | bytes 3010560 | tf_op jit(solution)/shard_map/all_gather | solution.py:29
  13.2 96.1 %copy-start.52 = (f32[128]{0:T(128)}, f32[128]{0:T(128)S(1)}, u32[]{:S(2)}) copy-start(f32[128]{0:T(128)S(1)} %convert_element_type.101) | copy-start | bytes 1540
  13.2 96.1 %copy-start.53 = (f32[128]{0:T(128)}, f32[128]{0:T(128)S(1)}, u32[]{:S(2)}) copy-start(f32[128]{0:T(128)S(1)} %convert_element_type.96) | copy-start | bytes 1540
  86.2 45.5 %copy-start.24 = (f32[2352,128]{1,0:T(8,128)}, f32[2352,128]{1,0:T(8,128)S(1)}, u32[]{:S(2)}) copy-start(f32[2352,128]{1,0:T(8,128)S(1)} %get-tuple-element.182) | copy-start | bytes 3612676
  86.3 24.9 %copy-start.67 = (bf16[128]{0:T(256)(128)(2,1)S(1)}, bf16[128]{0:T(256)(128)(2,1)}, u32[]{:S(2)}) copy-start(bf16[128]{0:T(256)(128)(2,1)} %param.43) | copy-start | bytes 772
  86.3 24.9 %copy-start.63 = (bf16[128]{0:T(256)(128)(2,1)S(1)}, bf16[128]{0:T(256)(128)(2,1)}, u32[]{:S(2)}) copy-start(bf16[128]{0:T(256)(128)(2,1)} %param.42) | copy-start | bytes 772
  109.3 27.4 %copy-start.39 = (f32[128]{0:T(128)}, f32[128]{0:T(128)S(1)}, u32[]{:S(2)}) copy-start(f32[128]{0:T(128)S(1)} %get-tuple-element.155) | copy-start | bytes 1540
  109.3 27.4 %copy-start.41 = (f32[128]{0:T(128)}, f32[128]{0:T(128)S(1)}, u32[]{:S(2)}) copy-start(f32[128]{0:T(128)S(1)} %get-tuple-element.156) | copy-start | bytes 1540
  110.6 136.9 %all-gather.8.cloned.1.call-start = ((), (), s32[]{:S(2)}) async-start(), calls=%async_computation.5 | async-start | bytes 3010560 | tf_op jit(solution)/shard_map/all_gather | solution.py:29
  111.2 113.9 %copy-start.54 = (f32[128]{0:T(128)}, f32[128]{0:T(128)S(1)}, u32[]{:S(2)}) copy-start(f32[128]{0:T(128)S(1)} %convert_element_type.103) | copy-start | bytes 1540
  111.2 113.9 %copy-start.56 = (f32[128]{0:T(128)}, f32[128]{0:T(128)S(1)}, u32[]{:S(2)}) copy-start(f32[128]{0:T(128)S(1)} %convert_element_type.95) | copy-start | bytes 1540
  177.6 20.6 %copy-start.3 = (bf16[2352,512]{1,0:T(8,128)(2,1)}, bf16[2352,512]{1,0:T(8,128)(2,1)S(1)}, u32[]{:S(2)}) copy-start(bf16[2352,512]{1,0:T(8,128)(2,1)S(1)} %reshape.575) | copy-start | bytes 7225348
  187.9 2.6 copy-start.11
  187.9 2.8 copy-start.28
  190.6 1.7 copy-start.13
  192.3 1.7 copy-start.7
  194.0 1.7 copy-start.1
  195.7 1.7 copy-start.9
  198.2 1.7 copy-start.5
  202.3 24.2 %copy-start.20 = (f32[2352,128]{1,0:T(8,128)}, f32[2352,128]{1,0:T(8,128)S(1)}, u32[]{:S(2)}) copy-start(f32[2352,128]{1,0:T(8,128)S(1)} %get-tuple-element.183) | copy-start | bytes 3612676
  202.3 24.1 %copy-start.59 = (bf16[512]{0:T(512)(128)(2,1)S(1)}, bf16[512]{0:T(512)(128)(2,1)}, u32[]{:S(2)}) copy-start(bf16[512]{0:T(512)(128)(2,1)} %param.46) | copy-start | bytes 3076
  202.3 24.1 %copy-start.50 = (bf16[512]{0:T(512)(128)(2,1)S(1)}, bf16[512]{0:T(512)(128)(2,1)}, u32[]{:S(2)}) copy-start(bf16[512]{0:T(512)(128)(2,1)} %param.45) | copy-start | bytes 3076
  202.4 45.2 %copy-start.33 = (bf16[512,512]{1,0:T(8,128)(2,1)S(1)}, bf16[512,512]{1,0:T(8,128)(2,1)}, u32[]{:S(2)}) copy-start(bf16[512,512]{1,0:T(8,128)(2,1)} %param.44) | copy-start | bytes 1572868
  225.1 27.9 %copy-start.43 = (f32[128]{0:T(128)}, f32[128]{0:T(128)S(1)}, u32[]{:S(2)}) copy-start(f32[128]{0:T(128)S(1)} %get-tuple-element.159) | copy-start | bytes 1540
  225.1 27.9 %copy-start.45 = (f32[128]{0:T(128)}, f32[128]{0:T(128)S(1)}, u32[]{:S(2)}) copy-start(f32[128]{0:T(128)S(1)} %get-tuple-element.160) | copy-start | bytes 1540
  226.4 171.2 %reduce-scatter.4.cloned.1.call-start = ((), (), s32[]{:S(2)}) async-start(), calls=%async_computation.6 | async-start | bytes 6021120 | tf_op jit(solution)/shard_map/reduce_scatter | solution.py:33
  226.5 64.8 %copy-start.60 = (f32[48]{0:T(128)}, f32[48]{0:T(128)S(1)}, u32[]{:S(2)}) copy-start(f32[48]{0:T(128)S(1)} %multiply_convert_fusion.6) | copy-start | bytes 580
  226.5 49.0 %copy-start.19 = (bf16[2352,512]{1,0:T(8,128)(2,1)S(1)}, bf16[2352,512]{1,0:T(8,128)(2,1)}, u32[]{:S(2)}) copy-start(bf16[2352,512]{1,0:T(8,128)(2,1)} %param.34) | copy-start | bytes 7225348
  303.9 5.0 copy-start.35
  304.8 4.1 copy-start.37
  314.9 25.9 %copy-start.47 = (f32[512]{0:T(512)S(1)}, f32[512]{0:T(512)}, u32[]{:S(2)}) copy-start(f32[512]{0:T(512)} %get-tuple-element.162) | copy-start | bytes 6148
  340.2 5.8 copy-start.51
  340.3 5.8 copy-start.58
  351.2 46.5 %copy-start.21 = (f32[2352,128]{1,0:T(8,128)S(1)}, f32[2352,128]{1,0:T(8,128)}, u32[]{:S(2)}) copy-start(f32[2352,128]{1,0:T(8,128)} %copy-done.20) | copy-start | bytes 3612676
  351.2 46.5 %copy-start.44 = (f32[128]{0:T(128)S(1)}, f32[128]{0:T(128)}, u32[]{:S(2)}) copy-start(f32[128]{0:T(128)} %copy-done.43) | copy-start | bytes 1540
  351.2 46.5 %copy-start.46 = (f32[128]{0:T(128)S(1)}, f32[128]{0:T(128)}, u32[]{:S(2)}) copy-start(f32[128]{0:T(128)} %copy-done.45) | copy-start | bytes 1540
  351.2 46.5 %copy-start.55 = (f32[128]{0:T(128)S(1)}, f32[128]{0:T(128)}, u32[]{:S(2)}) copy-start(f32[128]{0:T(128)} %copy-done.54) | copy-start | bytes 1540
  351.2 46.5 %copy-start.57 = (f32[128]{0:T(128)S(1)}, f32[128]{0:T(128)}, u32[]{:S(2)}) copy-start(f32[128]{0:T(128)} %copy-done.56) | copy-start | bytes 1540
  351.2 144.3 %reduce-scatter.6.cloned.1.call-start = ((), (), s32[]{:S(2)}) async-start(), calls=%async_computation.7 | async-start | bytes 6021120 | tf_op jit(solution)/shard_map/reduce_scatter | solution.py:33
  450.6 1.9 copy-start.68
  450.6 45.0 %copy-start.25 = (f32[2352,128]{1,0:T(8,128)S(1)}, f32[2352,128]{1,0:T(8,128)}, u32[]{:S(2)}) copy-start(f32[2352,128]{1,0:T(8,128)} %copy-done.24) | copy-start | bytes 3612676
  450.6 45.0 %copy-start.40 = (f32[128]{0:T(128)S(1)}, f32[128]{0:T(128)}, u32[]{:S(2)}) copy-start(f32[128]{0:T(128)} %copy-done.39) | copy-start | bytes 1540
  450.6 45.0 %copy-start.42 = (f32[128]{0:T(128)S(1)}, f32[128]{0:T(128)}, u32[]{:S(2)}) copy-start(f32[128]{0:T(128)} %copy-done.41) | copy-start | bytes 1540
  450.6 154.4 %reduce-scatter.8.cloned.1.call-start = ((), (), s32[]{:S(2)}) async-start(), calls=%async_computation.8 | async-start | bytes 12042240 | tf_op jit(solution)/shard_map/reduce_scatter | solution.py:50
  528.8 2.6 copy-start.23
  528.8 252.0 %all-reduce.12.cloned.1.call-start = ((), (), s32[]{:S(2)}) async-start(), calls=%async_computation.9 | async-start | bytes 9437184 | tf_op jit(solution)/shard_map/psum | solution.py:273
  531.5 4.5 copy-start.14
  535.9 2.2 copy-start.12
  538.2 2.3 copy-start.15
  540.4 1.8 copy-start.10
  541.3 2.0 copy-start.8
  543.3 1.7 copy-start.2
  545.0 1.7 copy-start.17
  545.8 1.9 copy-start.6
  547.7 1.7 copy-start.4
  559.6 31.9 %copy-start.49 = (f32[384]{0:T(512)S(1)}, f32[384]{0:T(512)}, u32[]{:S(2)}) copy-start(f32[384]{0:T(512)} %get-tuple-element.136) | copy-start | bytes 4612
  559.6 32.0 %copy-start.26 = (f32[4096,128]{1,0:T(8,128)S(1)}, f32[4096,128]{1,0:T(8,128)}, u32[]{:S(2)}) copy-start(f32[4096,128]{1,0:T(8,128)} %copy.92) | copy-start | bytes 6291460
  595.3 15.1 %copy-start.27 = (f32[4096,128]{1,0:T(8,128)}, f32[4096,128]{1,0:T(8,128)S(1)}, u32[]{:S(2)}) copy-start(f32[4096,128]{1,0:T(8,128)S(1)} %scatter_custom_fusion) | copy-start | bytes 6291460
  783.1 3.3 copy-start.32
  783.1 4.3 copy-start.34
  (14 other events, 13.5 us)
Sparse Core Ops, SparseCore 0:
  12.7 68.0 all-gather.3
  110.7 20.9 all-gather.5
  226.5 20.9 all-gather.7
  351.3 46.2 reduce-scatter.3
  450.7 44.7 reduce-scatter.5
  529.0 75.9 reduce-scatter.7
  610.1 170.7 all-reduce.11
where the time goes:
time: 800 us; the launch traced here: 795 us
  waiting for transfers between devices  375 us (47%)
  blocking collectives  168 us (21%)
  local copies, waits for them, and re-layouts  116 us (14%)
  matrix products  65.1 us (8%)
  other arithmetic  54.4 us (7%)
  between operations  15.9 us (2%)
    psum x1, waiting for transfers between devices, shards(): lax.psum((weight_terms[0], weight_terms[1], weight_terms[2], weight_terms...  170 us
    all_gather x3, waiting for transfers between devices, gather_narrow(): return lax.all_gather(value, 'narrow', axis=1, tiled=True)  108 us
    reduce_scatter x2, waiting for transfers between devices, reduce_narrow(): return lax.psum_scatter(value, 'narrow', scatter_dimension=1, tiled=True)  86.8 us
    psum x3, blocking collectives, sums_wide(): return lax.psum(values, 'wide')  65 us
    psum x3, blocking collectives, back_wide(): return lax.psum(values, 'wide')  61 us
    reshape x8, local copies, waits for them, and re-layouts, conv_forward(): window = padded[:, row_shift:row_shift + SIDE, column_shift:column_shift...  36.2 us
    all_gather x1, blocking collectives, shards(): lax.all_gather(embedding, 'wide', axis=0, tiled=True)  31.2 us
    unnamed x149, local copies, waits for them, and re-layouts  28.5 us
  transfers between devices with their start and end apart: 7, of which 7 were waited for; matrix products, arithmetic and copies ran while one was open for 5% of the time, Pallas kernels for 0%

commit v1 on v0

v1 whole, which is shorter than its diff:
```python
import functools

import jax
import jax.numpy as jnp
import numpy as np
from jax import lax
from jax.experimental import pallas as pl
from jax.experimental.pallas import tpu as pltpu
from jax.sharding import Mesh
from jax.sharding import PartitionSpec as P

SIDE = 7
SLOTS = SIDE * SIDE
GROUP = 8
ROWS = GROUP * SLOTS
EPS_NORM = 1e-05
EPS_EMBED = 1e-06
F32 = jnp.float32
BF16 = jnp.bfloat16
LANES = 128
OFFSETS = [(i - 1) * SIDE + (j - 1) for i in range(3) for j in range(3)]
ALL = ("wide", "hi", "lo")
VMEM_BYTES = 56 * 1024 * 1024


def tap_masks():
    row = (np.arange(ROWS) % SLOTS) // SIDE
    column = np.arange(ROWS) % SIDE
    kept = np.zeros((ROWS, 9), np.float32)
    for i in range(3):
        for j in range(3):
            r, c = row + i - 1, column + j - 1
            kept[:, 3 * i + j] = (r >= 0) & (r < SIDE) & (c >= 0) & (c < SIDE)
    return kept


def image_rows():
    image = np.arange(ROWS) // SLOTS
    return (image[None, :] == np.arange(GROUP)[:, None]).astype(np.float32)


def swap_lo(value):
    return lax.ppermute(value, "lo", [(0, 1), (1, 0)])


def swap_hi(value):
    return lax.ppermute(value, "hi", [(0, 1), (1, 0)])


def swap_both(value):
    return lax.ppermute(value, ("hi", "lo"), [(i, i ^ 3) for i in range(4)])


def spread(value, axes, copies):
    return lax.all_to_all(
        jnp.broadcast_to(value[None], (copies,) + value.shape), axes, 0, 0, tiled=True
    )


def sigmoid(value):
    return 1.0 / (1.0 + jnp.exp(-value))


def slope_of(value, sigma):
    return sigma * (1.0 + value * (1.0 - sigma))


def dot(left, right):
    return jnp.dot(left, right, preferred_element_type=F32)


def dot_nt(left, right):
    return lax.dot_general(left, right, (((1,), (1,)), ((), ())), preferred_element_type=F32)


def dot_tn(left, right):
    return lax.dot_general(left, right, (((0,), (0,)), ((), ())), preferred_element_type=F32)


def total_count(e_ref):
    e = e_ref[...]
    return jnp.sum(e.reshape(-1, 4, 8, LANES)[:, 0, 4:5, :], axis=0)


def set_sums(r_ref):
    r = r_ref[...]
    by_narrow = jnp.sum(r.reshape(-1, 4, 4, LANES), axis=0)
    sets = [by_narrow[k] + by_narrow[2 + k] for k in range(2)]
    return [(s[0:2], s[2:4]) for s in sets]


def flat(rows):
    return jnp.concatenate([rows[k : k + 1] for k in range(rows.shape[0])], axis=1)


def unflat(vector):
    return jnp.concatenate(
        [vector[:, k * LANES : (k + 1) * LANES] for k in range(vector.shape[1] // LANES)], axis=0
    )


class Norm:
    def __init__(self, sums, squares, count, gain, shift):
        self.mean = sums / count
        variance = squares / count - self.mean * self.mean
        self.scale = lax.rsqrt(variance + EPS_NORM)
        self.gain = gain
        self.shift = shift

    def normal(self, value):
        return (value - self.mean) * self.scale

    def apply(self, value):
        return self.gain * self.normal(value) + self.shift


def gains_of(e_ref, core, at):
    return jnp.concatenate([e_ref[core, at : at + 1], e_ref[2 + core, at : at + 1]], axis=1)


def mid_norms(e_ref, r_ref, at):
    count = total_count(e_ref)[:, :1]
    sums = set_sums(r_ref)
    return [
        Norm(
            flat(sums[core][0]),
            flat(sums[core][1]),
            count,
            gains_of(e_ref, core, at),
            gains_of(e_ref, core, at + 1),
        )
        for core in range(2)
    ], count


def choose(flag, first, second):
    return jnp.where(flag, first, second)


def choose_norm(flag, first, second):
    out = Norm.__new__(Norm)
    for name in ("mean", "scale", "gain", "shift"):
        setattr(out, name, jnp.where(flag, getattr(first, name), getattr(second, name)))
    return out


def half_norm(norm, second):
    out = Norm.__new__(Norm)
    for name in ("mean", "scale", "gain", "shift"):
        v = getattr(norm, name)
        setattr(out, name, jnp.where(second, v[:, LANES:], v[:, :LANES]))
    return out


def natural(set0, set1):
    return jnp.concatenate(
        [set0[:, :LANES], set1[:, :LANES], set0[:, LANES:], set1[:, LANES:]], axis=1
    )


def sets_of(value):
    return (
        jnp.concatenate([value[:, :LANES], value[:, 2 * LANES : 3 * LANES]], axis=1),
        jnp.concatenate([value[:, LANES : 2 * LANES], value[:, 3 * LANES :]], axis=1),
    )


def add_sums(st_ref, first, second, step):
    rows = jnp.concatenate([unflat(first), unflat(second)], axis=0)

    @pl.when(step == 0)
    def _():
        st_ref[...] = rows

    @pl.when(step > 0)
    def _():
        st_ref[...] += rows


def whole(shape):
    zero = (0,) * len(shape)
    return pl.BlockSpec(shape, lambda i, *_: zero)


def rows_spec(width, pick=None):
    if pick is None:
        return pl.BlockSpec((ROWS, width), lambda i, *_: (i, 0))
    return pl.BlockSpec((ROWS, width), pick)


def call(kernel, steps, in_specs, out_specs, out_shape, scratch=(), flops=0, bytes_moved=0, name=None):
    return pl.pallas_call(
        kernel,
        grid_spec=pltpu.PrefetchScalarGridSpec(
            num_scalar_prefetch=1,
            grid=(steps,),
            in_specs=in_specs,
            out_specs=out_specs,
            scratch_shapes=scratch,
        ),
        out_shape=out_shape,
        compiler_params=pltpu.CompilerParams(
            dimension_semantics=("arbitrary",), vmem_limit_bytes=VMEM_BYTES
        ),
        cost_estimate=pl.CostEstimate(flops=flops, bytes_accessed=bytes_moved, transcendentals=0),
        name=name,
    )


def one_kernel(at_ref, keep_ref, near_ref, far_ref, y_ref, st_ref):
    value = keep_ref[...] + near_ref[...].astype(F32) + far_ref[...].astype(F32)
    y_ref[...] = value.astype(BF16)
    add_sums(
        st_ref,
        jnp.sum(value, axis=0, keepdims=True),
        jnp.sum(value * value, axis=0, keepdims=True),
        pl.program_id(0),
    )


def conv_forward_kernel(at_ref, e_ref, r_ref, own_ref, near_ref, w_ref, mk_ref, y_ref, st_ref):
    norms, _ = mid_norms(e_ref, r_ref, 0)
    lo0 = at_ref[1] == 0
    inside = mk_ref[:, 9:10]
    own, near = own_ref[...].astype(F32), near_ref[...].astype(F32)
    halves = []
    for core in range(2):
        z = norms[core].apply(choose(lo0 if core == 0 else jnp.logical_not(lo0), own, near))
        halves.append(jnp.where(inside > 0, z * sigmoid(z), 0.0).astype(BF16))
    a = natural(halves[0], halves[1])
    total = jnp.zeros((ROWS, 2 * LANES), F32)
    for tap, offset in enumerate(OFFSETS):
        part = dot(a, w_ref[tap])
        if offset:
            part = pltpu.roll(part, (-offset) % ROWS, 0)
        total = total + part * mk_ref[:, tap : tap + 1]
    y_ref[...] = total.astype(BF16)
    kept = total * inside
    add_sums(
        st_ref,
        jnp.sum(kept, axis=0, keepdims=True),
        jnp.sum(kept * total, axis=0, keepdims=True),
        pl.program_id(0),
    )


def select_blocks(at_ref, refs, step, per_half):
    own, near, far, across = [ref[...].astype(F32) for ref in refs]
    mine = (step // per_half) == at_ref[0]
    a, b = choose(mine, own, far), choose(mine, near, across)
    lo0 = at_ref[1] == 0
    return choose(lo0, a, b), choose(lo0, b, a)


def third_kernel(per_half, at_ref, e_ref, r_ref, b0, b1, b2, b3, w_ref, mk_ref, a_ref, y_ref, st_ref):
    step = pl.program_id(0)
    norms, _ = mid_norms(e_ref, r_ref, 2)
    inside = mk_ref[:, 9:10]
    halves = []
    for norm, value in zip(norms, select_blocks(at_ref, (b0, b1, b2, b3), step, per_half)):
        z = norm.apply(value)
        halves.append(jnp.where(inside > 0, z * sigmoid(z), 0.0).astype(BF16))
    a = natural(halves[0], halves[1])
    a_ref[...] = a
    y = dot(a, w_ref[...])
    y_ref[...] = y
    add_sums(
        st_ref, jnp.sum(y, axis=0, keepdims=True), jnp.sum(y * y, axis=0, keepdims=True), step
    )


def third_norm(e_ref, r_ref, gb_ref):
    count = total_count(e_ref)[:, :1]
    sums = jnp.sum(r_ref[...], axis=0)
    return Norm(flat(sums[0:4]), flat(sums[4:8]), count, flat(gb_ref[0:4]), flat(gb_ref[4:8])), count


def split_low(value):
    high = value.astype(BF16)
    return high, (value - high.astype(F32)).astype(BF16)


def out_kernel(
    at_ref, e_ref, r_ref, gb_ref, y_ref, x_ref, og_ref, mk_ref, ind_ref, wh_ref,
    out_ref, pool_ref, s0_ref, s1_ref, raw_ref, st_ref,
):
    norm, _ = third_norm(e_ref, r_ref, gb_ref)
    inside = mk_ref[:, 9:10] > 0
    normal = norm.normal(y_ref[...])
    summed = jnp.where(
        inside, norm.gain * normal + norm.shift + x_ref[...].astype(F32), 0.0
    )
    sigma = sigmoid(summed)
    out = summed * sigma
    slope = jnp.where(inside, slope_of(summed, sigma), 0.0)
    out_ref[...] = out.astype(BF16)
    ind = ind_ref[...]
    high, low = split_low(out)
    pooled = ((dot(ind, high) + dot(ind, low)) / mk_ref[0:GROUP, 10:11]).astype(BF16)
    pool_ref[...] = pooled.astype(F32)
    sloped = slope * normal
    s0_ref[...] = dot(ind, slope.astype(BF16))
    s1_ref[...] = dot(ind, sloped.astype(BF16))
    raw_ref[...] = dot(pooled, wh_ref[...])
    og = og_ref[...].astype(F32)
    add_sums(
        st_ref,
        jnp.sum(og * slope, axis=0, keepdims=True),
        jnp.sum(og * sloped, axis=0, keepdims=True),
        pl.program_id(0),
    )


def head_kernel(
    at_ref, raw_ref, eg_ref, wh_ref, s0_ref, s1_ref, stl_ref, mk_ref,
    emb_ref, graw_ref, gp_ref, st_ref,
):
    raw, eg = raw_ref[...], eg_ref[...]
    inverse = lax.rsqrt(jnp.sum(raw * raw, axis=1, keepdims=True) + EPS_EMBED)
    emb = raw * inverse
    graw = (inverse * (eg - emb * jnp.sum(emb * eg, axis=1, keepdims=True))).astype(BF16)
    emb_ref[...] = emb
    graw_ref[...] = graw.astype(F32)
    gp = dot_nt(graw, wh_ref[...]) / mk_ref[0:1, 10:11]
    gp_ref[...] = gp
    add = jnp.concatenate(
        [
            unflat(jnp.sum(gp * s0_ref[...], axis=0, keepdims=True)),
            unflat(jnp.sum(gp * s1_ref[...], axis=0, keepdims=True)),
        ],
        axis=0,
    )
    st_ref[...] = stl_ref[...] + add


def back_three_kernel(
    at_ref, e_ref, r_ref, rb_ref, gb_ref, y_ref, x_ref, og_ref, gp_ref, mk_ref, ind_ref, w_ref,
    keep_ref, send_ref, gy_ref, dz_ref,
):
    norm, count = third_norm(e_ref, r_ref, gb_ref)
    back = jnp.sum(rb_ref[...], axis=0)
    d_shift, d_gain = flat(back[0:4]) / count, flat(back[4:8]) / count
    inside = mk_ref[:, 9:10] > 0
    normal = norm.normal(y_ref[...])
    summed = norm.gain * normal + norm.shift + x_ref[...].astype(F32)
    slope = jnp.where(inside, slope_of(summed, sigmoid(summed)), 0.0)
    high, low = split_low(gp_ref[...])
    ind = ind_ref[...]
    given = og_ref[...].astype(F32) + dot_tn(ind, high) + dot_tn(ind, low)
    dz = given * slope
    dz_ref[...] = dz.astype(BF16)
    gy = norm.gain * norm.scale * (dz - d_shift - normal * d_gain)
    gy = jnp.where(inside, gy, 0.0).astype(BF16)
    gy_ref[...] = gy
    set0, set1 = sets_of(dot_nt(gy, w_ref[...]))
    lo0 = at_ref[1] == 0
    keep_ref[...] = choose(lo0, set0, set1)
    send_ref[...] = choose(lo0, set1, set0).astype(BF16)


def slope_kernel(at, parts, at_ref, e_ref, r_ref, *refs):
    given, (y_ref, mk_ref, dz_ref, st_ref) = refs[:parts], refs[parts:]
    norms, _ = mid_norms(e_ref, r_ref, at)
    norm = choose_norm(at_ref[1] == 0, norms[0], norms[1])
    value = given[0][...].astype(F32)
    for ref in given[1:]:
        value = value + ref[...].astype(F32)
    normal = norm.normal(y_ref[...].astype(F32))
    z = norm.gain * normal + norm.shift
    dz = jnp.where(mk_ref[:, 9:10] > 0, value * slope_of(z, sigmoid(z)), 0.0)
    dz_ref[...] = dz.astype(BF16)
    add_sums(
        st_ref,
        jnp.sum(dz, axis=0, keepdims=True),
        jnp.sum(dz * normal, axis=0, keepdims=True),
        pl.program_id(0),
    )


def set_back(rb_ref, count):
    sums = set_sums(rb_ref)
    return [(flat(s[0]) / count, flat(s[1]) / count) for s in sums]


def grad_y(norm, dz, value, back, inside):
    gy = norm.gain * norm.scale * (dz - back[0] - norm.normal(value) * back[1])
    return jnp.where(inside, gy, 0.0)


def conv_input_kernel(
    at_ref, e_ref, r_ref, rb_ref, dz_ref, y_ref, w_ref, mk_ref, keep_ref, send_ref
):
    norms, count = mid_norms(e_ref, r_ref, 2)
    lo0 = at_ref[1] == 0
    norm = choose_norm(lo0, norms[0], norms[1])
    backs = set_back(rb_ref, count)
    back = [choose(lo0, backs[0][k], backs[1][k]) for k in range(2)]
    gy = grad_y(
        norm, dz_ref[...].astype(F32), y_ref[...].astype(F32), back, mk_ref[:, 9:10] > 0
    ).astype(BF16).astype(F32)
    total = jnp.zeros((ROWS, 4 * LANES), F32)
    for tap, offset in enumerate(OFFSETS):
        moved = pltpu.roll(gy, offset % ROWS, 0) if offset else gy
        moved = (moved * mk_ref[:, 8 - tap : 9 - tap]).astype(BF16)
        total = total + dot_nt(moved, w_ref[tap])
    set0, set1 = sets_of(total)
    keep_ref[...] = choose(lo0, set0, set1)
    send_ref[...] = choose(lo0, set1, set0).astype(BF16)


def conv_weight_kernel(
    per_half, at_ref, e_ref, r1_ref, r2_ref, rb_ref, b0, b1, b2, b3, dzo_ref, dzf_ref,
    yo_ref, yf_ref, mk_ref, gw_ref, acc_ref,
):
    step = pl.program_id(0)
    inside = mk_ref[:, 9:10]
    ones, count = mid_norms(e_ref, r1_ref, 0)
    halves = []
    for norm, value in zip(ones, select_blocks(at_ref, (b0, b1, b2, b3), step, per_half)):
        z = norm.apply(value)
        halves.append(jnp.where(inside > 0, z * sigmoid(z), 0.0).astype(BF16))
    a = natural(halves[0], halves[1])
    norms, _ = mid_norms(e_ref, r2_ref, 2)
    lo0, second = at_ref[1] == 0, at_ref[0] == 1
    norm = half_norm(choose_norm(lo0, norms[0], norms[1]), second)
    backs = set_back(rb_ref, count)
    back = [choose(lo0, backs[0][k], backs[1][k]) for k in range(2)]
    back = [choose(second, v[:, LANES:], v[:, :LANES]) for v in back]
    mine = (step // per_half) == at_ref[0]
    dz = choose(mine, dzo_ref[...].astype(F32), dzf_ref[...].astype(F32))
    y = choose(mine, yo_ref[...].astype(F32), yf_ref[...].astype(F32))
    gy = grad_y(norm, dz, y, back, inside > 0).astype(BF16).astype(F32)
    moved = []
    for tap, offset in enumerate(OFFSETS):
        part = pltpu.roll(gy, offset % ROWS, 0) if offset else gy
        moved.append((part * mk_ref[:, 8 - tap : 9 - tap]).astype(BF16))
    part = dot_tn(a, jnp.concatenate(moved, axis=1))

    @pl.when(step == 0)
    def _():
        acc_ref[...] = part

    @pl.when(step > 0)
    def _():
        acc_ref[...] += part

    @pl.when(step == pl.num_programs(0) - 1)
    def _():
        for tap in range(9):
            gw_ref[tap] = acc_ref[:, tap * LANES : (tap + 1) * LANES].astype(BF16)


def first_weight_kernel(
    per_half, at_ref, e_ref, r_ref, rb_ref, d0, d1, d2, d3, b0, b1, b2, b3, x_ref, mk_ref,
    gy_ref, gw_ref, acc_ref,
):
    step = pl.program_id(0)
    norms, count = mid_norms(e_ref, r_ref, 0)
    backs = set_back(rb_ref, count)
    inside = mk_ref[:, 9:10] > 0
    dzs = select_blocks(at_ref, (d0, d1, d2, d3), step, per_half)
    ys = select_blocks(at_ref, (b0, b1, b2, b3), step, per_half)
    halves = [
        grad_y(norms[k], dzs[k], ys[k], backs[k], inside).astype(BF16) for k in range(2)
    ]
    gy = natural(halves[0], halves[1])
    gy_ref[...] = gy
    part = dot_tn(x_ref[...], gy)

    @pl.when(step == 0)
    def _():
        acc_ref[...] = part

    @pl.when(step > 0)
    def _():
        acc_ref[...] += part

    @pl.when(step == pl.num_programs(0) - 1)
    def _():
        for block in range(4):
            gw_ref[block] = acc_ref[:, block * LANES : (block + 1) * LANES].astype(BF16)


def shards(
    n_wide,
    features,
    image_side,
    bank_slot,
    memory_bank,
    weight_one,
    gain_one,
    shift_one,
    weight_two,
    gain_two,
    shift_two,
    weight_three,
    gain_three,
    shift_three,
    weight_head,
    out_grad,
    embed_grad,
):
    hi, lo = lax.axis_index("hi"), lax.axis_index("lo")
    at = jnp.stack([hi, lo]).astype(jnp.int32)
    pixels, width = features.shape
    images = image_side.shape[0]
    half = pixels // 2
    per_half = half // ROWS
    steps = 2 * per_half
    n_all = 4 * n_wide
    hi0, lo0 = hi == 0, lo == 0
    side = image_side[0]

    position = jnp.arange(ROWS, dtype=jnp.int32)
    inside = (((position % SLOTS) // SIDE) < side) & ((position % SIDE) < side)
    count_img = (side * side).astype(F32)
    mk = jnp.concatenate(
        [
            jnp.asarray(tap_masks()),
            inside.astype(F32)[:, None],
            jnp.full((ROWS, 6), count_img, F32),
        ],
        axis=1,
    )
    ind = jnp.asarray(image_rows(), BF16)
    mk_spec, ind_spec = whole((ROWS, 16)), whole((GROUP, ROWS))
    e_spec, r_spec = whole((n_all, 8, LANES)), whole((n_all, 4, LANES))
    r3_spec, st_spec = whole((n_wide, 8, LANES)), whole((4, LANES))
    st_shape = jax.ShapeDtypeStruct((4, LANES), F32)

    rows_of = lambda h, l: lax.dynamic_slice_in_dim(weight_one, (2 * h + l) * width, width, 0)
    w_self = rows_of(hi, lo)
    w_near = swap_lo(rows_of(hi, 1 - lo))
    w_far = swap_hi(rows_of(1 - hi, lo))
    w_across = swap_both(rows_of(1 - hi, 1 - lo))

    small = jnp.concatenate(
        [
            gain_one.astype(F32)[None],
            shift_one.astype(F32)[None],
            gain_two.astype(F32)[None],
            shift_two.astype(F32)[None],
            jnp.full((1, LANES), count_img * images, F32),
            jnp.pad(bank_slot.astype(F32), (0, LANES - images))[None],
            jnp.zeros((2, LANES), F32),
        ],
        axis=0,
    )
    every = spread(small, ALL, n_all)
    gb3 = jnp.concatenate(
        [gain_three.astype(F32).reshape(4, LANES), shift_three.astype(F32).reshape(4, LANES)], 0
    )

    w_own = jnp.concatenate([jnp.where(hi0, w_self, w_far), jnp.where(hi0, w_far, w_self)], 1)
    w_oth = jnp.concatenate([jnp.where(hi0, w_near, w_across), jnp.where(hi0, w_across, w_near)], 1)
    w_set0, w_set1 = jnp.where(lo0, w_own, w_oth), jnp.where(lo0, w_oth, w_own)
    w_first = natural(w_set0, w_set1)
    w2_far = swap_hi(weight_two)
    w2 = jnp.concatenate(
        [jnp.where(hi0, weight_two, w2_far), jnp.where(hi0, w2_far, weight_two)], axis=3
    ).reshape(9, weight_two.shape[2], 2 * LANES)

    pixel_inside = jnp.tile(inside, steps)[:, None]
    masked = jnp.where(pixel_inside, features, jnp.zeros_like(features))
    near = swap_lo(dot(masked, w_oth).astype(BF16))
    keep = dot(masked, w_own)
    other_rows = (1 - hi) * half
    pick = lambda v: lax.dynamic_slice_in_dim(v, other_rows, half, 0)
    far = swap_hi((pick(keep) + pick(near).astype(F32)).astype(BF16))
    own_spec = rows_spec(2 * LANES, lambda i, at: (at[0] * per_half + i, 0))
    row_spec = rows_spec(2 * LANES)
    y_shape = jax.ShapeDtypeStruct((half, 2 * LANES), BF16)
    y1, st1 = call(
        one_kernel, per_half, [own_spec, own_spec, row_spec], [row_spec, st_spec],
        [y_shape, st_shape], bytes_moved=4 << 20, name="one",
    )(at, keep, near, far)
    y1_near = swap_lo(y1)
    r1 = spread(st1, ALL, n_all)

    w2_spec = whole(w2.shape)
    y2, st2 = call(
        conv_forward_kernel, per_half,
        [e_spec, r_spec, row_spec, row_spec, w2_spec, mk_spec], [row_spec, st_spec],
        [y_shape, st_shape], flops=18 * half * 512 * 256, bytes_moved=6 << 20, name="conv_forward",
    )(at, every, r1, y1, y1_near, w2, mk)
    y2_near = swap_lo(y2)
    y2_far = swap_hi(y2)
    r2 = spread(st2, ALL, n_all)
    y2_across = swap_lo(y2_far)

    y1_far = swap_hi(y1)
    y1_across = swap_lo(y1_far)

    part_spec = rows_spec(2 * LANES, lambda i, at: (i % per_half, 0))
    parts = [part_spec] * 4
    wide_spec = rows_spec(width)
    a2, y3, st3 = call(
        functools.partial(third_kernel, per_half), steps,
        [e_spec, r_spec] + parts + [whole(weight_three.shape), mk_spec],
        [wide_spec, wide_spec, whole((8, LANES))],
        [
            jax.ShapeDtypeStruct((pixels, 4 * LANES), BF16),
            jax.ShapeDtypeStruct((pixels, width), F32),
            jax.ShapeDtypeStruct((8, LANES), F32),
        ],
        flops=2 * pixels * 512 * width, bytes_moved=10 << 20, name="third",
    )(at, every, r2, y2, y2_near, y2_far, y2_across, weight_three, mk)
    r3 = spread(st3, "wide", n_wide)

    img_spec = pl.BlockSpec((GROUP, width), lambda i, *_: (i, 0))
    img_shape = jax.ShapeDtypeStruct((images, width), F32)
    gb_spec = whole((8, LANES))
    head_spec = whole(weight_head.shape)
    out, pooled, s0, s1, raw, st_local = call(
        out_kernel, steps,
        [e_spec, r3_spec, gb_spec, wide_spec, wide_spec, wide_spec, mk_spec, ind_spec, head_spec],
        [wide_spec, img_spec, img_spec, img_spec, pl.BlockSpec((GROUP, LANES), lambda i, *_: (i, 0)), whole((8, LANES))],
        [
            jax.ShapeDtypeStruct((pixels, width), BF16), img_shape, img_shape, img_shape,
            jax.ShapeDtypeStruct((images, LANES), F32), jax.ShapeDtypeStruct((8, LANES), F32),
        ],
        flops=8 * pixels * width, bytes_moved=12 << 20, name="out",
    )(at, every, r3, gb3, y3, features, out_grad, mk, ind, weight_head)
    raw = raw + swap_lo(raw)
    raw = raw + swap_hi(raw)
    small_spec = whole((images, LANES))
    all_img = whole((images, width))
    embedding, grad_raw, grad_pooled, st3b = call(
        head_kernel, 1,
        [small_spec, small_spec, head_spec, all_img, all_img, whole((8, LANES)), mk_spec],
        [small_spec, small_spec, all_img, whole((8, LANES))],
        [
            jax.ShapeDtypeStruct((images, LANES), F32), jax.ShapeDtypeStruct((images, LANES), F32),
            img_shape, jax.ShapeDtypeStruct((8, LANES), F32),
        ],
        bytes_moved=1 << 19, name="head",
    )(at, raw, embed_grad, weight_head, s0, s1, st_local, mk)
    r3b = spread(st3b, "wide", n_wide)

    set_spec = rows_spec(2 * LANES)
    ga_keep, ga_send, gy3, dz3 = call(
        back_three_kernel, steps,
        [e_spec, r3_spec, r3_spec, gb_spec, wide_spec, wide_spec, wide_spec, img_spec, mk_spec, ind_spec, whole(weight_three.shape)],
        [set_spec, set_spec, wide_spec, wide_spec],
        [
            jax.ShapeDtypeStruct((pixels, 2 * LANES), F32), jax.ShapeDtypeStruct((pixels, 2 * LANES), BF16),
            jax.ShapeDtypeStruct((pixels, width), BF16), jax.ShapeDtypeStruct((pixels, width), BF16),
        ],
        flops=2 * pixels * 512 * width, bytes_moved=16 << 20, name="back_three",
    )(at, every, r3, r3b, gb3, y3, features, out_grad, grad_pooled, mk, ind, weight_three)
    ga_near = swap_lo(ga_send)
    ga_far = swap_hi((pick(ga_keep) + pick(ga_near).astype(F32)).astype(BF16))
    dz2, st2b = call(
        functools.partial(slope_kernel, 2, 3), per_half,
        [e_spec, r_spec, own_spec, own_spec, row_spec, row_spec, mk_spec], [row_spec, st_spec],
        [y_shape, st_shape], bytes_moved=4 << 20, name="slope_two",
    )(at, every, r2, ga_keep, ga_near, ga_far, y2, mk)
    r2b = spread(st2b, ALL, n_all)

    gb_keep, gb_send = call(
        conv_input_kernel, per_half,
        [e_spec, r_spec, r_spec, row_spec, row_spec, w2_spec, mk_spec], [row_spec, row_spec],
        [jax.ShapeDtypeStruct((half, 2 * LANES), F32), y_shape],
        flops=18 * half * 512 * 256, bytes_moved=6 << 20, name="conv_input",
    )(at, every, r2, r2b, dz2, y2, w2, mk)
    gb_near = swap_lo(gb_send)
    dz1, st1b = call(
        functools.partial(slope_kernel, 0, 2), per_half,
        [e_spec, r_spec, row_spec, row_spec, row_spec, mk_spec], [row_spec, st_spec],
        [y_shape, st_shape], bytes_moved=3 << 20, name="slope_one",
    )(at, every, r1, gb_keep, gb_near, y1, mk)
    dz1_near = swap_lo(dz1)
    dz1_far = swap_hi(dz1)
    r1b = spread(st1b, ALL, n_all)
    dz1_across = swap_lo(dz1_far)

    theirs = jnp.where(hi0, dz2[:, LANES:], dz2[:, :LANES])
    mine = jnp.where(hi0, dz2[:, :LANES], dz2[:, LANES:])
    dz2_far = swap_hi(theirs)
    lane_part = pl.BlockSpec((ROWS, LANES), lambda i, at: (i % per_half, 0))
    lane_pick = pl.BlockSpec((ROWS, LANES), lambda i, at: (i % per_half, at[0]))
    grad_two = call(
        functools.partial(conv_weight_kernel, per_half), steps,
        [e_spec, r_spec, r_spec, r_spec] + parts + [lane_part, lane_part, lane_pick, lane_pick, mk_spec],
        whole((9, 512, LANES)), jax.ShapeDtypeStruct((9, 512, LANES), BF16),
        scratch=[pltpu.VMEM((512, 9 * LANES), F32)],
        flops=18 * pixels * 512 * LANES, bytes_moved=8 << 20, name="conv_weight",
    )(at, every, r1, r2, r2b, y1, y1_near, y1_far, y1_across, mine, dz2_far, y2, y2_far, mk)

    gy1, grad_one = call(
        functools.partial(first_weight_kernel, per_half), steps,
        [e_spec, r_spec, r_spec] + parts + parts + [wide_spec, mk_spec],
        [rows_spec(4 * LANES), whole((4, width, LANES))],
        [jax.ShapeDtypeStruct((pixels, 4 * LANES), BF16), jax.ShapeDtypeStruct((4, width, LANES), BF16)],
        scratch=[pltpu.VMEM((width, 4 * LANES), F32)],
        flops=2 * pixels * 512 * width, bytes_moved=8 << 20, name="first_weight",
    )(at, every, r1, r1b, dz1, dz1_near, dz1_far, dz1_across, y1, y1_near, y1_far, y1_across, features, mk)
    grad_features = (dot_nt(gy1, w_first) + dz3.astype(F32)).astype(BF16)

    piece = width // n_wide
    sent = grad_one.reshape(4, n_wide, piece, LANES).transpose(1, 0, 2, 3).reshape(n_all, piece, LANES)
    got = lax.all_to_all(sent, ALL, 0, 0, tiled=True).astype(F32)
    got = jnp.sum(got.reshape(n_wide, 4, piece, LANES), axis=0).astype(BF16)
    grad_one = (
        spread(got, "wide", n_wide).reshape(n_wide, 4, piece, LANES)
        .transpose(1, 0, 2, 3).reshape(4 * width, LANES).astype(F32)
    )
    grad_two = lax.psum(grad_two, "wide").astype(F32).reshape(weight_two.shape)
    grad_three = dot_tn(a2, gy3).astype(BF16)
    grad_head = dot_tn(pooled.astype(BF16), grad_raw.astype(BF16)).astype(BF16)
    grad_three, grad_head = lax.psum((grad_three, grad_head), "wide")

    def own_sums(r):
        by = jnp.sum(r.reshape(n_wide, 2, 2, 2, 2, LANES), axis=(0, 1))
        both = lax.dynamic_index_in_dim(by, lo, 0, keepdims=False)
        both = lax.dynamic_index_in_dim(both, hi, 1, keepdims=False)
        return both[0], both[1]

    d_shift_one, d_gain_one = own_sums(r1b)
    d_shift_two, d_gain_two = own_sums(r2b)
    back_three = jnp.sum(r3b, axis=0)
    d_shift_three, d_gain_three = back_three[:4].reshape(-1), back_three[4:].reshape(-1)

    all_embed = spread(embedding, "wide", n_wide).reshape(-1, LANES)
    all_slot = every.reshape(n_wide, 4, 8, LANES)[:, 0, 5, :images].reshape(-1)
    bank_rows = memory_bank.shape[0]
    owner = all_slot.astype(jnp.int32) - lax.axis_index("wide") * bank_rows
    owned = (owner >= 0) & (owner < bank_rows)
    target = jnp.where(owned, owner, bank_rows)
    previous = jnp.take(memory_bank, jnp.minimum(target, bank_rows - 1), axis=0)
    mixed = 0.5 * previous + 0.5 * all_embed
    mixed = mixed * lax.rsqrt(jnp.sum(mixed * mixed, axis=1, keepdims=True) + EPS_EMBED)
    new_bank = memory_bank.at[target].set(mixed, mode="drop")

    return (
        out,
        embedding,
        grad_features,
        grad_one,
        d_gain_one,
        d_shift_one,
        grad_two,
        d_gain_two,
        d_shift_two,
        grad_three.astype(F32),
        d_gain_three,
        d_shift_three,
        grad_head.astype(F32),
        new_bank,
    )


def solution(mesh):
    n_wide, n_narrow = mesh.shape["wide"], mesh.shape["narrow"]
    split = Mesh(mesh.devices.reshape(n_wide, n_narrow // 2, 2), ALL)
    narrow = ("hi", "lo")
    in_specs = (
        P("wide", narrow),
        P("wide"),
        P("wide"),
        P("wide", None),
        P(None, narrow),
        P(narrow),
        P(narrow),
        P(None, None, None, narrow),
        P(narrow),
        P(narrow),
        P(None, narrow),
        P(narrow),
        P(narrow),
        P(narrow, None),
        P("wide", narrow),
        P("wide", None),
    )
    out_specs = (
        P("wide", narrow),
        P("wide", None),
        P("wide", narrow),
        P(None, narrow),
        P(narrow),
        P(narrow),
        P(None, None, None, narrow),
        P(narrow),
        P(narrow),
        P(None, narrow),
        P(narrow),
        P(narrow),
        P(narrow, None),
        P("wide", None),
    )
    return jax.shard_map(
        functools.partial(shards, n_wide),
        mesh=split,
        in_specs=in_specs,
        out_specs=out_specs,
        check_vma=False,
    )
```

time: 800 us -> 435 us (0.54)
  waiting for transfers between devices: 375 us -> 190 us
  blocking collectives: 168 us -> 29.2 us
  Pallas kernels: 0 us -> 91.1 us
  local copies, waits for them, and re-layouts: 116 us -> 29.8 us
  matrix products: 65.1 us -> 14.4 us
  starting transfers between devices: 0.81 us -> 42.7 us
  other arithmetic: 54.4 us -> 20.5 us
    psum x7 -> x0, blocking collectives: 136 us -> none  [the longest x3 65 us: sums_wide(): return lax.psum(values, 'wide')]
    all_gather x3 -> x0, waiting for transfers between devices: 108 us -> none  [gather_narrow(): return lax.all_gather(value, 'narrow', axis=1, tiled=True)]
    reduce_scatter x3 -> x0, waiting for transfers between devices: 96.4 us -> none  [the longest x2 86.8 us: reduce_narrow(): return lax.psum_scatter(value, 'narrow', scatter_dimension=1, tiled=True)]
    pallas_call x0 -> x11, Pallas kernels: none -> 91.1 us  [the longest x1 15.9 us: shards(): call(functools.partial(conv_weight_kernel, per_half), steps, [e_spec, r_s...]
    ppermute x0 -> x21, waiting for transfers between devices: none -> 87.1 us  [the longest x9 78.3 us: swap_hi(): return lax.ppermute(value, 'hi', [(0, 1), (1, 0)])]
    psum x1, waiting for transfers between devices: 170 us -> 91.1 us  [shards(): grad_two = lax.psum(grad_two, 'wide').astype(F32).reshape(weight_two.shape)]
    reshape x12 -> x2, local copies, waits for them, and re-layouts: 59.2 us -> 2.46 us  [the longest x1 1.88 us: shards(): grad_one.reshape(4, n_wide, piece, LANES).transpose(1, 0, 2, 3)]
    dot_general x36 -> x5, matrix products: 65.1 us -> 14.4 us  [the longest x2 5.66 us: dot_tn(): lax.dot_general(left, right, (((0,), (0,)), ((), ())), preferred_element_...]
  transfers between devices with their start and end apart: 7 -> 29, of which waited for: 7 -> 14; matrix products, arithmetic and copies ran while one was open for 5% -> 10% of each run, Pallas kernels for 0% -> 8%
where the time goes in v1:
time: 435 us; the launch traced here: 433 us
  waiting for transfers between devices  190 us (44%)
  Pallas kernels  91.1 us (21%)
  starting transfers between devices  42.7 us (10%)
  local copies, waits for them, and re-layouts  29.8 us (7%)
  blocking collectives  29.2 us (7%)
  other arithmetic  20.5 us (5%)
  between operations  14.8 us (3%)
  matrix products  14.4 us (3%)
    psum x1, waiting for transfers between devices, shards(): grad_two = lax.psum(grad_two, 'wide').astype(F32).reshape(weight_two.shape)  91.1 us
    ppermute x9, waiting for transfers between devices, swap_hi(): return lax.ppermute(value, 'hi', [(0, 1), (1, 0)])  78.3 us
    all_to_all x3, blocking collectives, spread(): lax.all_to_all(jnp.broadcast_to(value[None], (copies,) + value.shape), ax...  29.2 us
    all_to_all x6, starting transfers between devices, spread(): lax.all_to_all(jnp.broadcast_to(value[None], (copies,) + value.shape), ax...  25.8 us
    pallas_call x1, Pallas kernels, shards(): call(functools.partial(conv_weight_kernel, per_half), steps, [e_spec, r_s...  15.9 us
    unnamed x93, local copies, waits for them, and re-layouts  12.1 us
    pallas_call x1, Pallas kernels, shards(): call(back_three_kernel, steps, [e_spec, r3_spec, r3_spec, gb_spec, wide_s...  11.8 us
    all_to_all x6, waiting for transfers between devices, spread(): lax.all_to_all(jnp.broadcast_to(value[None], (copies,) + value.shape), ax...  11.7 us
  transfers between devices with their start and end apart: 29, of which 14 were waited for; matrix products, arithmetic and copies ran while one was open for 10% of the time, Pallas kernels for 8%

profile of v1, /device:TPU:0, one launch (start us, length us, event | category | flops | bytes accessed | tf_op | source)
XLA Modules:
  0.0 432.6 jit_solution(5199843448948908205)
XLA Ops:
  7.2 3.2 copy.62
  11.5 2.6 collective-permute-start.2
  14.4 3.7 collective-permute-done.2
  18.1 2.4 convolution_convert_fusion
  20.6 1.5 collective-permute-start
  22.7 4.4 %collective-permute-done = bf16[512,128]{1,0:T(8,128)(2,1)} collective-permute-done((bf16[512,128]{1,0:T(8,128)(2,1)S(1)}, bf16[512,128]{1,0:T(8,128)(2,1)}, u32[]{:S(2)}, u32[]{:S(2)}) %collective-permute-start) | collective-permute-done | bytes 131104 | tf_op jit(solution)/shard_map/ppermute | solution.py:47
  27.1 1.0 broadcast_select_fusion.12
  28.0 0.8 fusion.1.keep_ref
  29.0 1.3 copy-done.3
  30.3 1.2 add_convert_fusion.1
  31.6 1.7 collective-permute-start.4
  34.1 4.9 %all-to-all-start = ((f32[32,8,128]{2,1,0:T(8,128)}), f32[32,8,128]{2,1,0:T(8,128)S(1)}, u32[]{:S(2)}, u32[]{:S(2)}) async-start(f32[32,8,128]{2,1,0:T(8,128)} %broadcast_in_dim.133), calls=%async_computation | async-start | bytes 262144 | tf_op jit(solution)/shard_map/all_to_all | solution.py:55
  39.7 26.2 %collective-permute-done.4.far_ref = bf16[1176,256]{1,0:T(8,128)(2,1)S(1)} collective-permute-done((bf16[1176,256]{1,0:T(8,128)(2,1)S(1)}, bf16[1176,256]{1,0:T(8,128)(2,1)S(1)}, u32[]{:S(2)}, u32[]{:S(2)}) %collective-permute-start.4) | collective-permute-done | bytes 602144 | tf_op jit(solution)/shard_map/ppermute | solution.py:47
  65.9 0.8 copy-done.12
  66.7 4.0 one.1
  71.7 1.8 broadcast_select_fusion.2
  74.1 5.6 %all-to-all-start.1 = ((f32[32,4,128]{2,1,0:T(4,128)}), f32[32,4,128]{2,1,0:T(4,128)S(1)}, u32[]{:S(2)}, u32[]{:S(2)}) async-start(f32[32,4,128]{2,1,0:T(4,128)} %broadcast_in_dim.137), calls=%async_computation.1 | async-start | bytes 131072 | tf_op jit(solution)/shard_map/all_to_all | solution.py:55
  79.8 1.7 pad_maximum_fusion
  81.4 5.7 %all-to-all-done.1.r_ref.r1_ref = f32[32,4,128]{2,1,0:T(4,128)S(1)} async-done(((f32[32,4,128]{2,1,0:T(4,128)}), f32[32,4,128]{2,1,0:T(4,128)S(1)}, u32[]{:S(2)}, u32[]{:S(2)}) %all-to-all-start.1) | async-done | bytes 65568 | tf_op jit(solution)/shard_map/all_to_all | solution.py:55
  88.0 7.9 %conv_forward.1 = (bf16[1176,256]{1,0:T(8,128)(2,1)}, f32[4,128]{1,0:T(4,128)}) custom-call(s32[2]{0:T(128)} %pad_add_fusion.at_ref, f32[32,8,128]{2,1,0:T(8,128)} %copy-done.4, f32[32,4,128]{2,1,0:T(4,128)} %copy-done.16, bf16[1176,256]{1,0:T(8,128)(2,1)} %get-tuple-element.44.own_ref.refs_2_.b0, bf16[1176,256]{1,0:T(8,128)(2,1)} %copy-done.7, ...), custom_call_target="tpu_custom_call" | custom-call | flops 2774532096 | bytes 6291456 | tf_op jit(solution)/shard_map/conv_forward/pallas_call | solution.py:581
  96.4 15.4 %collective-permute-done.8.b2.yf_ref = bf16[1176,256]{1,0:T(8,128)(2,1)S(1)} collective-permute-done((bf16[1176,256]{1,0:T(8,128)(2,1)}, bf16[1176,256]{1,0:T(8,128)(2,1)S(1)}, u32[]{:S(2)}, u32[]{:S(2)}) %collective-permute-start.8) | collective-permute-done | bytes 602144 | tf_op jit(solution)/shard_map/ppermute | solution.py:47
  112.5 9.7 %all_to_all.50.r_ref.r2_ref = f32[32,4,128]{2,1,0:T(4,128)} all-to-all(f32[32,4,128]{2,1,0:T(4,128)S(1)} %broadcast_in_dim.139), channel_id=1, replica_groups=mesh['wide'=8,'hi'=2,'lo'=2] {'wide','hi','lo'}, dimensions={0} | all-to-all | bytes 131072 | tf_op jit(solution)/shard_map/all_to_all | solution.py:55
  123.1 0.8 copy-done.44
  123.9 10.0 %third.1 = (bf16[2352,512]{1,0:T(8,128)(2,1)}, f32[2352,512]{1,0:T(8,128)}, f32[8,128]{1,0:T(8,128)}) custom-call(s32[2]{0:T(128)} %pad_add_fusion.at_ref, f32[32,8,128]{2,1,0:T(8,128)} %copy-done.4, f32[32,4,128]{2,1,0:T(4,128)} %all_to_all.50.r_ref.r2_ref, bf16[1176,256]{1,0:T(8,128)(2,1)} %get-tuple-element.46.b0.refs_3_.y_ref.yo_ref, ...), custom_call_target="tpu_custom_call" | custom-call | flops 1233125376 | bytes 10485760 | tf_op jit(solution)/shard_map/third/pallas_call | solution.py:597
  133.9 1.3 broadcast_in_dim.140
  135.2 3.3 all-to-all-start.3
  139.2 6.0 %all-to-all-done.3.r_ref = f32[8,8,128]{2,1,0:T(8,128)S(1)} async-done(((f32[8,8,128]{2,1,0:T(8,128)}), f32[8,8,128]{2,1,0:T(8,128)S(1)}, u32[]{:S(2)}, u32[]{:S(2)}) %all-to-all-start.3) | async-done | bytes 32800 | tf_op jit(solution)/shard_map/all_to_all | solution.py:55
  145.8 10.5 %out.1 = (bf16[2352,512]{1,0:T(8,128)(2,1)}, f32[48,512]{1,0:T(8,128)}, f32[48,512]{1,0:T(8,128)}, f32[48,512]{1,0:T(8,128)}, f32[48,128]{1,0:T(8,128)}, /*index=5*/f32[8,128]{1,0:T(8,128)}) custom-call(s32[2]{0:T(128)} %pad_add_fusion.at_ref, f32[32,8,128]{2,1,0:T(8,128)} %copy-done.4, f32[8,8,128]{2,1,0:T(8,128)} %copy-done.25, ...), custom_call_target="tpu_custom_call" | custom-call | flops 9633792 | bytes 12582912 | tf_op jit(solution)/shard_map/out/pallas_call | solution.py:614
  156.4 1.4 collective-permute-done.10
  159.0 3.4 collective-permute-done.11
  163.0 2.7 head.1
  166.3 9.7 %all_to_all.51.rb_ref = f32[8,8,128]{2,1,0:T(8,128)} all-to-all(f32[8,8,128]{2,1,0:T(8,128)S(1)} %broadcast_in_dim.141), channel_id=1, replica_groups=mesh['wide'=8,'hi'=2,'lo'=2] {'wide'}, dimensions={0} | all-to-all | bytes 65536 | tf_op jit(solution)/shard_map/all_to_all | solution.py:55
  176.1 11.8 %back_three.1 = (f32[2352,256]{1,0:T(8,128)}, bf16[2352,256]{1,0:T(8,128)(2,1)}, bf16[2352,512]{1,0:T(8,128)(2,1)}, bf16[2352,512]{1,0:T(8,128)(2,1)}) custom-call(s32[2]{0:T(128)} %pad_add_fusion.at_ref, f32[32,8,128]{2,1,0:T(8,128)} %copy-done.4, f32[8,8,128]{2,1,0:T(8,128)} %copy-done.25, f32[8,8,128]{2,1,0:T(8,128)} %all_to_all.51.rb_ref, ...), custom_call_target="tpu_custom_call" | custom-call | flops 1233125376 | bytes 16777216 | tf_op jit(solution)/shard_map/back_three/pallas_call | solution.py:641
  187.9 3.1 collective-permute-done.12.refs_1_
  191.0 1.9 add_convert_fusion
  193.4 15.2 %collective-permute-done.13.refs_2_ = bf16[1176,256]{1,0:T(8,128)(2,1)S(1)} collective-permute-done((bf16[1176,256]{1,0:T(8,128)(2,1)S(1)}, bf16[1176,256]{1,0:T(8,128)(2,1)S(1)}, u32[]{:S(2)}, u32[]{:S(2)}) %collective-permute-start.13) | collective-permute-done | bytes 602144 | tf_op jit(solution)/shard_map/ppermute | solution.py:47
  208.6 0.8 copy-done.15
  209.4 4.9 %slope_two.1 = (bf16[1176,256]{1,0:T(8,128)(2,1)}, f32[4,128]{1,0:T(4,128)}) custom-call(s32[2]{0:T(128)} %pad_add_fusion.at_ref, f32[32,8,128]{2,1,0:T(8,128)} %copy-done.4, f32[32,4,128]{2,1,0:T(4,128)} %all_to_all.50.r_ref.r2_ref, f32[2352,256]{1,0:T(8,128)} %get-tuple-element.57.refs_0_, bf16[2352,256]{1,0:T(8,128)(2,1)} %copy-done.5, ...), custom_call_target="tpu_custom_call" | custom-call | bytes 4194304 | tf_op jit(solution)/shard_map/slope_two/pallas_call | solution.py:653
  215.0 9.8 %all_to_all.52.rb_ref = f32[32,4,128]{2,1,0:T(4,128)} all-to-all(f32[32,4,128]{2,1,0:T(4,128)S(1)} %broadcast_in_dim.142), channel_id=1, replica_groups=mesh['wide'=8,'hi'=2,'lo'=2] {'wide','hi','lo'}, dimensions={0} | all-to-all | bytes 131072 | tf_op jit(solution)/shard_map/all_to_all | solution.py:55
  224.8 7.5 %conv_input.1 = (f32[1176,256]{1,0:T(8,128)}, bf16[1176,256]{1,0:T(8,128)(2,1)}) custom-call(s32[2]{0:T(128)} %pad_add_fusion.at_ref, f32[32,8,128]{2,1,0:T(8,128)} %copy-done.4, f32[32,4,128]{2,1,0:T(4,128)} %all_to_all.50.r_ref.r2_ref, f32[32,4,128]{2,1,0:T(4,128)} %all_to_all.52.rb_ref, bf16[1176,256]{1,0:T(8,128)(2,1)} %get-tuple-element.60.dz_ref, ...), custom_call_target="tpu_custom_call" | custom-call | flops 2774532096 | bytes 6291456 | tf_op jit(solution)/shard_map/conv_input/pallas_call | solution.py:660
  235.4 4.7 %slope_one.1 = (bf16[1176,256]{1,0:T(8,128)(2,1)}, f32[4,128]{1,0:T(4,128)}) custom-call(s32[2]{0:T(128)} %pad_add_fusion.at_ref, f32[32,8,128]{2,1,0:T(8,128)} %copy-done.4, f32[32,4,128]{2,1,0:T(4,128)} %copy-done.16, f32[1176,256]{1,0:T(8,128)} %get-tuple-element.61.refs_0_, bf16[1176,256]{1,0:T(8,128)(2,1)} %copy-done.14, ...), custom_call_target="tpu_custom_call" | custom-call | bytes 3145728 | tf_op jit(solution)/shard_map/slope_one/pallas_call | solution.py:667
  240.1 0.9 collective-permute-start.16
  241.5 1.4 fusion.34
  243.1 5.9 %collective-permute-done.18.b2 = bf16[1176,256]{1,0:T(8,128)(2,1)S(1)} collective-permute-done((bf16[1176,256]{1,0:T(8,128)(2,1)S(1)}, bf16[1176,256]{1,0:T(8,128)(2,1)S(1)}, u32[]{:S(2)}, u32[]{:S(2)}) %collective-permute-start.18) | collective-permute-done | bytes 602144 | tf_op jit(solution)/shard_map/ppermute | solution.py:47
  249.0 0.9 convolution_convert_fusion.2
  250.4 1.3 broadcast_in_dim.143
  251.7 2.6 all-to-all-start.6
  254.3 7.8 %collective-permute-done.16.d2 = bf16[1176,256]{1,0:T(8,128)(2,1)S(1)} collective-permute-done((bf16[1176,256]{1,0:T(8,128)(2,1)}, bf16[1176,256]{1,0:T(8,128)(2,1)S(1)}, u32[]{:S(2)}, u32[]{:S(2)}) %collective-permute-start.16) | collective-permute-done | bytes 602144 | tf_op jit(solution)/shard_map/ppermute | solution.py:47
  262.1 2.2 broadcast_select_fusion.5
  265.5 3.4 all-to-all-start.9
  268.9 4.8 %convolution_convert_fusion.1 = bf16[512,512]{1,0:T(8,128)(2,1)} fusion(bf16[2352,512]{1,0:T(8,128)(2,1)} %get-tuple-element.68, bf16[2352,512]{1,0:T(8,128)(2,1)} %get-tuple-element.69), kind=kOutput, calls=%fused_computation.7 | convolution fusion | flops 1233387520 | bytes 5341184 | tf_op jit(solution)/shard_map/dot_general | solution.py:77
  275.5 11.1 %first_weight.1 = (bf16[2352,512]{1,0:T(8,128)(2,1)}, bf16[4,512,128]{2,1,0:T(8,128)(2,1)}) custom-call(s32[2]{0:T(128)} %pad_add_fusion.at_ref, f32[32,8,128]{2,1,0:T(8,128)} %copy-done.4, f32[32,4,128]{2,1,0:T(4,128)} %copy-done.16, f32[32,4,128]{2,1,0:T(4,128)} %copy-done.17, bf16[1176,256]{1,0:T(8,128)(2,1)} %get-tuple-element.64.d0, ...), custom_call_target="tpu_custom_call" | custom-call | flops 1233125376 | bytes 8388608 | tf_op jit(solution)/shard_map/first_weight/pallas_call | solution.py:690
  286.6 1.9 copy.53
  288.5 6.0 %all-to-all-start.7 = ((bf16[32,64,128]{2,1,0:T(8,128)(2,1)}), bf16[32,64,128]{2,1,0:T(8,128)(2,1)S(1)}, u32[]{:S(2)}, u32[]{:S(2)}) async-start(bf16[32,64,128]{2,1,0:T(8,128)(2,1)} %bitcast.13), calls=%async_computation.7 | async-start | bytes 1048576 | tf_op jit(solution)/shard_map/all_to_all | solution.py:702
  294.7 15.9 %conv_weight.1 = bf16[9,512,128]{2,1,0:T(8,128)(2,1)} custom-call(s32[2]{0:T(128)} %pad_add_fusion.at_ref, f32[32,8,128]{2,1,0:T(8,128)} %copy-done.4, f32[32,4,128]{2,1,0:T(4,128)} %copy-done.16, f32[32,4,128]{2,1,0:T(4,128)} %all_to_all.50.r_ref.r2_ref, f32[32,4,128]{2,1,0:T(4,128)} %all_to_all.52.rb_ref, ...), custom_call_target="tpu_custom_call" | custom-call | flops 2774532096 | bytes 8388608 | tf_op jit(solution)/shard_map/conv_weight/pallas_call | solution.py:682
  310.6 1.1 gather_fusion
  312.8 0.9 broadcast_in_dim.144
  313.7 5.9 %all-to-all-start.8 = ((bf16[8,4,64,128]{3,2,1,0:T(8,128)(2,1)}), bf16[8,4,64,128]{3,2,1,0:T(8,128)(2,1)S(1)}, u32[]{:S(2)}, u32[]{:S(2)}) async-start(bf16[8,4,64,128]{3,2,1,0:T(8,128)(2,1)} %broadcast_in_dim.144), calls=%async_computation.8 | async-start | bytes 1048576 | tf_op jit(solution)/shard_map/all_to_all | solution.py:55
  319.8 2.2 scatter_fusion
  323.3 5.5 %fusion = bf16[2352,512]{1,0:T(8,128)(2,1)} fusion(bf16[2352,512]{1,0:T(8,128)(2,1)} %get-tuple-element.66, bf16[2352,512]{1,0:T(8,128)(2,1)} %get-tuple-element.65, bf16[512,128]{1,0:T(8,128)(2,1)} %get-tuple-element.106, bf16[512,128]{1,0:T(8,128)(2,1)} %get-tuple-element.91, bf16[512,128]{1,0:T(8,128)(2,1)} %get-tuple-element.107, ...), kind=kOutput, calls=%fused_computation.3 | convolution fusion | flops 1238835200 | bytes 7749632 | tf_op jit(solution)/shard_map/dot_general | solution.py:73
  328.7 91.1 %all-reduce.4.cloned.1.call-done = (bf16[3,3,512,128]{3,2,1,0:T(8,128)(2,1)}, bf16[512,512]{1,0:T(8,128)(2,1)}, bf16[512,128]{1,0:T(8,128)(2,1)}) async-done(((bf16[3,3,512,128]{3,2,1,0:T(8,128)(2,1)}, bf16[512,512]{1,0:T(8,128)(2,1)}, bf16[512,128]{1,0:T(8,128)(2,1)}), (bf16[3,3,512,128]{3,2,1,0:T(8,128)(2,1)}, bf16[512,512]{1,0:T(8,128)(2,1)}, bf16[512,128]{1,0:T(8,128)(2,1)})) %all-reduce.4.cloned.1.call-update) | async-done | bytes 1835024 | tf_op jit(solution)/shard_map/psum | solution.py:708
  419.9 2.9 reshape.303
  422.8 1.1 convert_element_type.116
  424.6 1.1 copy_convert_fusion
  (171 shorter events, 23.2 us)
Async XLA Ops:
  7.2 3.2 copy-start.20
  7.2 7.0 %copy-start.37 = (s32[48]{0:T(128)S(1)}, s32[48]{0:T(128)}, u32[]{:S(2)}) copy-start(s32[48]{0:T(128)} %param.19) | copy-start | bytes 580
  7.2 10.9 %copy-start = (bf16[2352,512]{1,0:T(8,128)(2,1)S(1)}, bf16[2352,512]{1,0:T(8,128)(2,1)}, u32[]{:S(2)}) copy-start(bf16[2352,512]{1,0:T(8,128)(2,1)} %x_ref.5) | copy-start | bytes 7225348
  11.1 3.3 collective-permute-start.1
  11.5 6.5 %collective-permute-start.2 = (bf16[512,128]{1,0:T(8,128)(2,1)S(1)}, bf16[512,128]{1,0:T(8,128)(2,1)S(1)}, u32[]{:S(2)}, u32[]{:S(2)}) collective-permute-start(bf16[512,128]{1,0:T(8,128)(2,1)S(1)} %get-tuple-element.89), channel_id=1, source_target_pairs={{0,3},{1,2},{2,1},{3,0},{4,7},{5,6},{6,5},{7,4},{8,11},{9,10},{10,... | collective-permute-start | bytes 393224 | tf_op jit(solution)/shard_map/ppermute | solution.py:51
  18.1 2.5 copy-start.29
  20.5 8.5 %collective-permute-start.3 = (bf16[2352,256]{1,0:T(8,128)(2,1)}, bf16[2352,256]{1,0:T(8,128)(2,1)}, u32[]{:S(2)}, u32[]{:S(2)}) collective-permute-start(bf16[2352,256]{1,0:T(8,128)(2,1)} %convolution_convert_fusion), channel_id=1, source_target_pairs={{0,1},{1,0},{2,3},{3,2},{4,5},{5,4},{6,7},{7,6},{8,9},{9,8},{10,11... | collective-permute-start | bytes 3612680 | tf_op jit(solution)/shard_map/ppermute | solution.py:43
  20.6 6.5 %collective-permute-start = (bf16[512,128]{1,0:T(8,128)(2,1)S(1)}, bf16[512,128]{1,0:T(8,128)(2,1)}, u32[]{:S(2)}, u32[]{:S(2)}) collective-permute-start(bf16[512,128]{1,0:T(8,128)(2,1)S(1)} %copy-done.29), channel_id=1, source_target_pairs={{0,2},{2,0},{1,3},{3,1},{4,6},{6,4},{5,7},{7,5},{8,10},{10,8},{9,1... | collective-permute-start | bytes 393224 | tf_op jit(solution)/shard_map/ppermute | solution.py:47
  22.1 49.5 %collective-permute-start.6 = (bf16[3,3,512,128]{3,2,1,0:T(8,128)(2,1)}, bf16[3,3,512,128]{3,2,1,0:T(8,128)(2,1)}, u32[]{:S(2)}, u32[]{:S(2)}) collective-permute-start(bf16[3,3,512,128]{3,2,1,0:T(8,128)(2,1)} %param.25), channel_id=1, source_target_pairs={{0,2},{2,0},{1,3},{3,1},{4,6},{6,4},{5,7},{7,5},{8,10},{10,8},{9,1... | collective-permute-start | bytes 3538952 | tf_op jit(solution)/shard_map/ppermute | solution.py:47
  28.0 0.9 copy-start.21
  28.9 1.4 copy-start.3
  28.9 4.3 copy-start.38
  28.9 4.3 copy-start.39
  28.9 4.3 %copy-start.45 = (s32[48]{0:T(128)S(1)}, s32[48]{0:T(128)}, u32[]{:S(2)}) copy-start(s32[48]{0:T(128)} %param.20) | copy-start | bytes 580
  29.0 4.4 %copy-start.40 = (bf16[128]{0:T(256)(128)(2,1)S(1)}, bf16[128]{0:T(256)(128)(2,1)}, u32[]{:S(2)}) copy-start(bf16[128]{0:T(256)(128)(2,1)} %param.27) | copy-start | bytes 772
  29.0 4.4 %copy-start.41 = (bf16[128]{0:T(256)(128)(2,1)S(1)}, bf16[128]{0:T(256)(128)(2,1)}, u32[]{:S(2)}) copy-start(bf16[128]{0:T(256)(128)(2,1)} %param.26) | copy-start | bytes 772
  31.6 39.2 %copy-start.31 = (f32[392,9]{0,1:T(8,128)S(1)}, f32[392,9]{0,1:T(8,128)}, u32[]{:S(2)}) copy-start(f32[392,9]{0,1:T(8,128)} %constant.139.clone) | copy-start | bytes 42340
  31.6 34.3 %collective-permute-start.4 = (bf16[1176,256]{1,0:T(8,128)(2,1)S(1)}, bf16[1176,256]{1,0:T(8,128)(2,1)S(1)}, u32[]{:S(2)}, u32[]{:S(2)}) collective-permute-start(bf16[1176,256]{1,0:T(8,128)(2,1)S(1)} %add_convert_fusion.1), channel_id=1, source_target_pairs={{0,2},{2,0},{1,3},{3,1},{4,6},{6,4},{5,7},{7,5},{8,10},{10,8},{9,1... | collective-permute-start | bytes 1806344 | tf_op jit(solution)/shard_map/ppermute | solution.py:47
  34.1 39.4 %all-to-all-start = ((f32[32,8,128]{2,1,0:T(8,128)}), f32[32,8,128]{2,1,0:T(8,128)S(1)}, u32[]{:S(2)}, u32[]{:S(2)}) async-start(f32[32,8,128]{2,1,0:T(8,128)} %broadcast_in_dim.133), calls=%async_computation | async-start | bytes 262144 | tf_op jit(solution)/shard_map/all_to_all | solution.py:55
  70.8 16.4 %collective-permute-start.5 = (bf16[1176,256]{1,0:T(8,128)(2,1)}, bf16[1176,256]{1,0:T(8,128)(2,1)S(1)}, u32[]{:S(2)}, u32[]{:S(2)}) collective-permute-start(bf16[1176,256]{1,0:T(8,128)(2,1)} %get-tuple-element.44.own_ref.refs_2_.b0), channel_id=1, source_target_pairs={{0,1},{1,0},{2,3},{3,2},{4,5},{5,4},{6,7},{7,6},{8,9},{9,8},{10,11... | collective-permute-start | bytes 1806344 | tf_op jit(solution)/shard_map/ppermute | solution.py:43
  71.7 1.8 copy-start.34
  73.5 8.0 %copy-start.4 = (f32[32,8,128]{2,1,0:T(8,128)}, f32[32,8,128]{2,1,0:T(8,128)S(1)}, u32[]{:S(2)}) copy-start(f32[32,8,128]{2,1,0:T(8,128)S(1)} %all-to-all-done.e_ref) | copy-start | bytes 393220
  74.1 13.0 %all-to-all-start.1 = ((f32[32,4,128]{2,1,0:T(4,128)}), f32[32,4,128]{2,1,0:T(4,128)S(1)}, u32[]{:S(2)}, u32[]{:S(2)}) async-start(f32[32,4,128]{2,1,0:T(4,128)} %broadcast_in_dim.137), calls=%async_computation.1 | async-start | bytes 131072 | tf_op jit(solution)/shard_map/all_to_all | solution.py:55
  95.9 15.8 %collective-permute-start.8 = (bf16[1176,256]{1,0:T(8,128)(2,1)}, bf16[1176,256]{1,0:T(8,128)(2,1)S(1)}, u32[]{:S(2)}, u32[]{:S(2)}) collective-permute-start(bf16[1176,256]{1,0:T(8,128)(2,1)} %get-tuple-element.46.b0.refs_3_.y_ref.yo_ref), channel_id=1, source_target_pairs={{0,2},{2,0},{1,3},{3,1},{4,6},{6,4},{5,7},{7,5},{8,10},{10,8},{9,1... | collective-permute-start | bytes 1806344 | tf_op jit(solution)/shard_map/ppermute | solution.py:47
  96.4 25.9 %collective-permute-start.7 = (bf16[1176,256]{1,0:T(8,128)(2,1)}, bf16[1176,256]{1,0:T(8,128)(2,1)S(1)}, u32[]{:S(2)}, u32[]{:S(2)}) collective-permute-start(bf16[1176,256]{1,0:T(8,128)(2,1)} %get-tuple-element.46.b0.refs_3_.y_ref.yo_ref), channel_id=1, source_target_pairs={{0,1},{1,0},{2,3},{3,2},{4,5},{5,4},{6,7},{7,6},{8,9},{9,8},{10,11... | collective-permute-start | bytes 1806344 | tf_op jit(solution)/shard_map/ppermute | solution.py:43
  111.8 10.5 %copy-start.42 = (bf16[1176,256]{1,0:T(8,128)(2,1)}, bf16[1176,256]{1,0:T(8,128)(2,1)S(1)}, u32[]{:S(2)}) copy-start(bf16[1176,256]{1,0:T(8,128)(2,1)S(1)} %collective-permute-done.8.b2.yf_ref) | copy-start | bytes 1806340
  111.8 10.5 %collective-permute-start.9 = (bf16[1176,256]{1,0:T(8,128)(2,1)S(1)}, bf16[1176,256]{1,0:T(8,128)(2,1)S(1)}, u32[]{:S(2)}, u32[]{:S(2)}) collective-permute-start(bf16[1176,256]{1,0:T(8,128)(2,1)S(1)} %collective-permute-done.8.b2.yf_ref), channel_id=1, source_target_pairs={{0,1},{1,0},{2,3},{3,2},{4,5},{5,4},{6,7},{7,6},{8,9},{9,8},{10,11... | collective-permute-start | bytes 1806344 | tf_op jit(solution)/shard_map/ppermute | solution.py:43
  112.5 26.1 %copy-start.35 = (bf16[512]{0:T(512)(128)(2,1)S(1)}, bf16[512]{0:T(512)(128)(2,1)}, u32[]{:S(2)}) copy-start(bf16[512]{0:T(512)(128)(2,1)} %param.30) | copy-start | bytes 3076
  112.5 26.1 %copy-start.36 = (bf16[512]{0:T(512)(128)(2,1)S(1)}, bf16[512]{0:T(512)(128)(2,1)}, u32[]{:S(2)}) copy-start(bf16[512]{0:T(512)(128)(2,1)} %param.29) | copy-start | bytes 3076
  135.2 10.0 %all-to-all-start.3 = ((f32[8,8,128]{2,1,0:T(8,128)}), f32[8,8,128]{2,1,0:T(8,128)S(1)}, u32[]{:S(2)}, u32[]{:S(2)}) async-start(f32[8,8,128]{2,1,0:T(8,128)} %broadcast_in_dim.140), calls=%async_computation.3 | async-start | bytes 65536 | tf_op jit(solution)/shard_map/all_to_all | solution.py:55
  156.3 1.5 collective-permute-start.10
  158.5 3.8 collective-permute-start.11
  187.9 3.2 collective-permute-start.12
  191.0 17.6 %copy-start.5 = (bf16[2352,256]{1,0:T(8,128)(2,1)}, bf16[2352,256]{1,0:T(8,128)(2,1)S(1)}, u32[]{:S(2)}) copy-start(bf16[2352,256]{1,0:T(8,128)(2,1)S(1)} %collective-permute-done.12.refs_1_) | copy-start | bytes 3612676
  192.9 15.7 %collective-permute-start.13 = (bf16[1176,256]{1,0:T(8,128)(2,1)S(1)}, bf16[1176,256]{1,0:T(8,128)(2,1)S(1)}, u32[]{:S(2)}, u32[]{:S(2)}) collective-permute-start(bf16[1176,256]{1,0:T(8,128)(2,1)S(1)} %add_convert_fusion), channel_id=1, source_target_pairs={{0,2},{2,0},{1,3},{3,1},{4,6},{6,4},{5,7},{7,5},{8,10},{10,8},{9,1... | collective-permute-start | bytes 1806344 | tf_op jit(solution)/shard_map/ppermute | solution.py:47
  224.8 7.6 %copy-start.22 = (bf16[512,128]{1,0:T(8,128)(2,1)S(1)}, bf16[512,128]{1,0:T(8,128)(2,1)}, u32[]{:S(2)}) copy-start(bf16[512,128]{1,0:T(8,128)(2,1)} %copy-done.21) | copy-start | bytes 393220
  224.8 7.6 %copy-start.24 = (bf16[512,128]{1,0:T(8,128)(2,1)S(1)}, bf16[512,128]{1,0:T(8,128)(2,1)}, u32[]{:S(2)}) copy-start(bf16[512,128]{1,0:T(8,128)(2,1)} %copy-done.23) | copy-start | bytes 393220
  224.8 7.7 %copy-start.6 = (bf16[1176,256]{1,0:T(8,128)(2,1)S(1)}, bf16[1176,256]{1,0:T(8,128)(2,1)}, u32[]{:S(2)}) copy-start(bf16[1176,256]{1,0:T(8,128)(2,1)} %get-tuple-element.44.own_ref.refs_2_.b0) | copy-start | bytes 1806340
  232.3 2.2 collective-permute-start.14
  232.4 16.6 %copy-start.30 = (f32[48,512]{1,0:T(8,128)S(1)}, f32[48,512]{1,0:T(8,128)}, u32[]{:S(2)}) copy-start(f32[48,512]{1,0:T(8,128)} %get-tuple-element.70) | copy-start | bytes 294916
  232.4 16.6 %copy-start.33 = (f32[48,128]{1,0:T(8,128)S(1)}, f32[48,128]{1,0:T(8,128)}, u32[]{:S(2)}) copy-start(f32[48,128]{1,0:T(8,128)} %get-tuple-element.71) | copy-start | bytes 73732
  232.6 16.5 %collective-permute-start.18 = (bf16[1176,256]{1,0:T(8,128)(2,1)S(1)}, bf16[1176,256]{1,0:T(8,128)(2,1)S(1)}, u32[]{:S(2)}, u32[]{:S(2)}) collective-permute-start(bf16[1176,256]{1,0:T(8,128)(2,1)S(1)} %copy-done.6), channel_id=1, source_target_pairs={{0,2},{2,0},{1,3},{3,1},{4,6},{6,4},{5,7},{7,5},{8,10},{10,8},{9,1... | collective-permute-start | bytes 1806344 | tf_op jit(solution)/shard_map/ppermute | solution.py:47
  233.9 30.9 %copy-start.32 = (f32[48,128]{1,0:T(8,128)S(1)}, f32[48,128]{1,0:T(8,128)}, u32[]{:S(2)}) copy-start(f32[48,128]{1,0:T(8,128)} %get-tuple-element.30) | copy-start | bytes 73732
  240.1 22.0 %collective-permute-start.16 = (bf16[1176,256]{1,0:T(8,128)(2,1)}, bf16[1176,256]{1,0:T(8,128)(2,1)S(1)}, u32[]{:S(2)}, u32[]{:S(2)}) collective-permute-start(bf16[1176,256]{1,0:T(8,128)(2,1)} %get-tuple-element.64.d0), channel_id=1, source_target_pairs={{0,2},{2,0},{1,3},{3,1},{4,6},{6,4},{5,7},{7,5},{8,10},{10,8},{9,1... | collective-permute-start | bytes 1806344 | tf_op jit(solution)/shard_map/ppermute | solution.py:47
  249.0 24.6 %copy-start.8 = (bf16[1176,256]{1,0:T(8,128)(2,1)}, bf16[1176,256]{1,0:T(8,128)(2,1)S(1)}, u32[]{:S(2)}) copy-start(bf16[1176,256]{1,0:T(8,128)(2,1)S(1)} %collective-permute-done.18.b2) | copy-start | bytes 1806340
  249.0 24.6 %collective-permute-start.19 = (bf16[1176,256]{1,0:T(8,128)(2,1)S(1)}, bf16[1176,256]{1,0:T(8,128)(2,1)S(1)}, u32[]{:S(2)}, u32[]{:S(2)}) collective-permute-start(bf16[1176,256]{1,0:T(8,128)(2,1)S(1)} %collective-permute-done.18.b2), channel_id=1, source_target_pairs={{0,1},{1,0},{2,3},{3,2},{4,5},{5,4},{6,7},{7,6},{8,9},{9,8},{10,11... | collective-permute-start | bytes 1806344 | tf_op jit(solution)/shard_map/ppermute | solution.py:43
  249.9 23.8 %collective-permute-start.15 = (bf16[1176,256]{1,0:T(8,128)(2,1)}, bf16[1176,256]{1,0:T(8,128)(2,1)S(1)}, u32[]{:S(2)}, u32[]{:S(2)}) collective-permute-start(bf16[1176,256]{1,0:T(8,128)(2,1)} %get-tuple-element.64.d0), channel_id=1, source_target_pairs={{0,1},{1,0},{2,3},{3,2},{4,5},{5,4},{6,7},{7,6},{8,9},{9,8},{10,11... | collective-permute-start | bytes 1806344 | tf_op jit(solution)/shard_map/ppermute | solution.py:43
  251.7 13.0 %all-to-all-start.6 = ((f32[32,4,128]{2,1,0:T(4,128)}), f32[32,4,128]{2,1,0:T(4,128)S(1)}, u32[]{:S(2)}, u32[]{:S(2)}) async-start(f32[32,4,128]{2,1,0:T(4,128)} %broadcast_in_dim.143), calls=%async_computation.6 | async-start | bytes 131072 | tf_op jit(solution)/shard_map/all_to_all | solution.py:55
  262.1 11.5 %copy-start.10 = (bf16[1176,256]{1,0:T(8,128)(2,1)}, bf16[1176,256]{1,0:T(8,128)(2,1)S(1)}, u32[]{:S(2)}) copy-start(bf16[1176,256]{1,0:T(8,128)(2,1)S(1)} %collective-permute-done.16.d2) | copy-start | bytes 1806340
  262.1 11.6 %collective-permute-start.17 = (bf16[1176,256]{1,0:T(8,128)(2,1)S(1)}, bf16[1176,256]{1,0:T(8,128)(2,1)S(1)}, u32[]{:S(2)}, u32[]{:S(2)}) collective-permute-start(bf16[1176,256]{1,0:T(8,128)(2,1)S(1)} %collective-permute-done.16.d2), channel_id=1, source_target_pairs={{0,1},{1,0},{2,3},{3,2},{4,5},{5,4},{6,7},{7,6},{8,9},{9,8},{10,11... | collective-permute-start | bytes 1806344 | tf_op jit(solution)/shard_map/ppermute | solution.py:43
  264.3 30.3 %collective-permute-start.20 = (bf16[1176,128]{1,0:T(8,128)(2,1)}, bf16[1176,128]{1,0:T(8,128)(2,1)}, u32[]{:S(2)}, u32[]{:S(2)}) collective-permute-start(bf16[1176,128]{1,0:T(8,128)(2,1)} %get-tuple-element.83), channel_id=1, source_target_pairs={{0,2},{2,0},{1,3},{3,1},{4,6},{6,4},{5,7},{7,5},{8,10},{10,8},{9,1... | collective-permute-start | bytes 903176 | tf_op jit(solution)/shard_map/ppermute | solution.py:47
  264.8 8.9 %copy-start.17 = (f32[32,4,128]{2,1,0:T(4,128)}, f32[32,4,128]{2,1,0:T(4,128)S(1)}, u32[]{:S(2)}) copy-start(f32[32,4,128]{2,1,0:T(4,128)S(1)} %all-to-all-done.6.rb_ref) | copy-start | bytes 196612
  265.5 23.1 %all-to-all-start.9 = ((f32[8,48,128]{2,1,0:T(8,128)}), f32[8,48,128]{2,1,0:T(8,128)S(1)}, u32[]{:S(2)}, u32[]{:S(2)}) async-start(f32[8,48,128]{2,1,0:T(8,128)} %broadcast_in_dim.147), calls=%async_computation.9 | async-start | bytes 393216 | tf_op jit(solution)/shard_map/all_to_all | solution.py:55
  273.7 1.0 copy-start.11
  288.5 24.2 %all-to-all-start.7 = ((bf16[32,64,128]{2,1,0:T(8,128)(2,1)}), bf16[32,64,128]{2,1,0:T(8,128)(2,1)S(1)}, u32[]{:S(2)}, u32[]{:S(2)}) async-start(bf16[32,64,128]{2,1,0:T(8,128)(2,1)} %bitcast.13), calls=%async_computation.7 | async-start | bytes 1048576 | tf_op jit(solution)/shard_map/all_to_all | solution.py:702
  294.6 125.3 %all-reduce.4.cloned.1.call-start = ((), (), s32[]{:S(2)}) async-start(), calls=%async_computation.10 | async-start | bytes 3670016 | tf_op jit(solution)/shard_map/psum | solution.py:708
  294.6 15.9 %copy-start.1 = (f32[4096,128]{1,0:T(8,128)S(1)}, f32[4096,128]{1,0:T(8,128)}, u32[]{:S(2)}) copy-start(f32[4096,128]{1,0:T(8,128)} %copy.62) | copy-start | bytes 6291460
  310.5 1.2 copy-start.26
  313.7 8.4 %copy-start.27 = (f32[32,4,128]{2,1,0:T(4,128)S(1)}, f32[32,4,128]{2,1,0:T(4,128)}, u32[]{:S(2)}) copy-start(f32[32,4,128]{2,1,0:T(4,128)} %all_to_all.52.rb_ref) | copy-start | bytes 196612
  313.7 9.0 %copy-start.18 = (f32[32,4,128]{2,1,0:T(4,128)S(1)}, f32[32,4,128]{2,1,0:T(4,128)}, u32[]{:S(2)}) copy-start(f32[32,4,128]{2,1,0:T(4,128)} %copy-done.17) | copy-start | bytes 196612
  313.7 110.9 %all-to-all-start.8 = ((bf16[8,4,64,128]{3,2,1,0:T(8,128)(2,1)}), bf16[8,4,64,128]{3,2,1,0:T(8,128)(2,1)S(1)}, u32[]{:S(2)}, u32[]{:S(2)}) async-start(bf16[8,4,64,128]{3,2,1,0:T(8,128)(2,1)} %broadcast_in_dim.144), calls=%async_computation.8 | async-start | bytes 1048576 | tf_op jit(solution)/shard_map/all_to_all | solution.py:55
  322.0 6.7 %copy-start.2 = (f32[4096,128]{1,0:T(8,128)}, f32[4096,128]{1,0:T(8,128)S(1)}, u32[]{:S(2)}) copy-start(f32[4096,128]{1,0:T(8,128)S(1)} %scatter_fusion) | copy-start | bytes 6291460
  419.9 2.9 copy-start.19
  419.9 4.0 copy-start.28
  (11 other events, 8.7 us)
Sparse Core Ops, SparseCore 0:
  310.7 109.1 all-reduce.3
